TPU v7x, 256 devices: a whole 4x4x8 slice. The times are simulated.
256 devices in a mesh: enc: 16 (over z, core), seq: 16 (over y, x).
Axes of the slice: x: 4, y: 4, z: 8, core: 2. Of those that a mesh axis runs over, the one named last changes fastest.
Arguments:
- queries: bfloat16 [16, 2048, 8192], P('enc', 'seq'), may hold values from -160 to 160
- kv_pool: bfloat16 [128, 2, 128, 8192], P('enc', None, None, 'seq'), may hold values from -16 to 16
- send_lists: int32 [16, 16, 1], P('enc'), may hold values from 0 to 7, as said below
- block_slots: int32 [16, 32, 2], P('enc'), may hold values from 0 to 15, as said below
- grad_context: bfloat16 [16, 2048, 8192], P('enc', 'seq'), may hold values from -24 to 24
Outputs:
- context: bfloat16 [16, 2048, 8192], P('enc', 'seq')
- grad_queries: bfloat16 [16, 2048, 8192], P('enc', 'seq')
- grad_pool: bfloat16 [128, 2, 128, 8192], P('enc', None, None, 'seq')
Inputs may be any that keep to these rules, and one draw needn't show every extreme that they name: send_lists[o, e] names 1 different local entries; each of a shard's 8 entries is named for at least one sequence. `block_slots`: the two slots of a block differ; every slot of a sequence is named by at least one of its blocks.
All inputs are finite; a program needn't handle non-finite values.
Results may differ from a plain program's by a relative error of at most 0.0065.
Values may be sent and summed in bfloat16 or wider, within the bound.
A program may use at most 128 MiB of HBM per device.

v0:
```python
import jax
import jax.numpy as jnp
from jax import lax
from jax.sharding import PartitionSpec as P

DH = 128
BLOCK = 64
NBLEN = 128


def to_heads(token_major):
    return lax.all_to_all(token_major, "seq", split_axis=2, concat_axis=1, tiled=True)


def to_tokens(head_major):
    return lax.all_to_all(head_major, "seq", split_axis=1, concat_axis=2, tiled=True)


def fetch_slots(kv_pool, entries):
    outgoing = kv_pool[entries]
    arrived = lax.all_to_all(outgoing, "enc", split_axis=0, concat_axis=0, tiled=True)
    return arrived.reshape((-1,) + kv_pool.shape[1:])


def move_up(row_data):
    filler = jnp.zeros((BLOCK - 1, row_data.shape[1]), row_data.dtype)
    return jnp.concatenate([row_data[BLOCK - 1 :], filler], axis=0)


def move_down(row_data):
    filler = jnp.zeros((BLOCK - 1, row_data.shape[1]), row_data.dtype)
    return jnp.concatenate([filler, row_data[: row_data.shape[0] - BLOCK + 1]], axis=0)


def into_blocks(head_rows, heads_here):
    blocks = head_rows.shape[0] // BLOCK
    return move_up(head_rows).reshape(blocks, BLOCK, heads_here, DH).transpose(0, 2, 1, 3)


def out_of_blocks(block_rows):
    blocks, heads_here = (block_rows.shape[0], block_rows.shape[1])
    return move_down(block_rows.transpose(0, 2, 1, 3).reshape(blocks * BLOCK, heads_here * DH))


def forward_parts(head_rows, arrived, block_use):
    slots = arrived.shape[0]
    heads_here = arrived.shape[-1] // DH
    queries_moved = into_blocks(head_rows, heads_here)
    pool_heads = arrived.reshape(slots, 2, NBLEN, heads_here, DH).transpose(0, 1, 3, 2, 4)
    keys_used = [pool_heads[:, 0][block_use[:, 0]], pool_heads[:, 0][block_use[:, 1]]]
    values_used = [pool_heads[:, 1][block_use[:, 0]], pool_heads[:, 1][block_use[:, 1]]]
    scores = [
        jnp.einsum("chid,chjd->chij", queries_moved, keys, preferred_element_type=jnp.float32)
        * DH ** (-0.5)
        for keys in keys_used
    ]
    row_peak = jnp.maximum(
        jnp.max(scores[0], axis=-1, keepdims=True), jnp.max(scores[1], axis=-1, keepdims=True)
    )
    weights = [jnp.exp(part_scores - row_peak) for part_scores in scores]
    total = jnp.sum(weights[0], axis=-1, keepdims=True) + jnp.sum(
        weights[1], axis=-1, keepdims=True
    )
    row_probs = [part_weights / total for part_weights in weights]
    probs_low = [part_probs.astype(jnp.bfloat16) for part_probs in row_probs]
    return (queries_moved, keys_used, values_used, row_probs, probs_low)


def local(queries, kv_pool, send_lists, block_slots, grad_context):
    block_use = block_slots[0]
    entries = send_lists[0]
    head_width = kv_pool.shape[-1]
    heads_here = head_width // DH
    score_scale = DH ** (-0.5)
    arrived = fetch_slots(kv_pool, entries)
    slots = arrived.shape[0]
    queries_moved, keys_used, values_used, row_probs, probs_low = forward_parts(
        to_heads(queries)[0], arrived, block_use
    )
    out_blocks = jnp.einsum(
        "chij,chjd->chid", probs_low[0], values_used[0], preferred_element_type=jnp.float32
    )
    out_blocks = out_blocks + jnp.einsum(
        "chij,chjd->chid", probs_low[1], values_used[1], preferred_element_type=jnp.float32
    )
    context = to_tokens(out_of_blocks(out_blocks.astype(jnp.bfloat16))[None])
    head_grads = to_heads(grad_context)[0]
    grads_moved = into_blocks(head_grads, heads_here)
    grad_probs = [
        jnp.einsum("chid,chjd->chij", grads_moved, values, preferred_element_type=jnp.float32)
        for values in values_used
    ]
    row_inner = jnp.sum(row_probs[0] * grad_probs[0], axis=-1, keepdims=True) + jnp.sum(
        row_probs[1] * grad_probs[1], axis=-1, keepdims=True
    )
    grad_scores = [
        (row_probs[n] * (grad_probs[n] - row_inner) * score_scale).astype(jnp.bfloat16)
        for n in range(2)
    ]
    query_grads = jnp.einsum(
        "chij,chjd->chid", grad_scores[0], keys_used[0], preferred_element_type=jnp.float32
    )
    query_grads = query_grads + jnp.einsum(
        "chij,chjd->chid", grad_scores[1], keys_used[1], preferred_element_type=jnp.float32
    )
    grad_queries = to_tokens(out_of_blocks(query_grads.astype(jnp.bfloat16))[None])
    slot_range = jnp.arange(slots, dtype=jnp.int32)
    slot_key = jnp.zeros((slots, heads_here, NBLEN, DH), jnp.float32)
    slot_value = jnp.zeros((slots, heads_here, NBLEN, DH), jnp.float32)
    for n in range(2):
        picker = (block_use[:, n][:, None] == slot_range[None, :]).astype(jnp.bfloat16)
        key_part = jnp.einsum(
            "chij,chid->chjd", grad_scores[n], queries_moved, preferred_element_type=jnp.float32
        ).astype(jnp.bfloat16)
        value_part = jnp.einsum(
            "chij,chid->chjd", probs_low[n], grads_moved, preferred_element_type=jnp.float32
        ).astype(jnp.bfloat16)
        slot_key = slot_key + jnp.einsum(
            "cs,chjd->shjd", picker, key_part, preferred_element_type=jnp.float32
        )
        slot_value = slot_value + jnp.einsum(
            "cs,chjd->shjd", picker, value_part, preferred_element_type=jnp.float32
        )
    slot_grads = jnp.stack([slot_key.astype(jnp.bfloat16), slot_value.astype(jnp.bfloat16)], axis=1)
    slot_grads = slot_grads.transpose(0, 1, 3, 2, 4).reshape(slots, 2, NBLEN, head_width)
    returned = lax.all_to_all(
        slot_grads.reshape(entries.shape + slot_grads.shape[1:]),
        "enc",
        split_axis=0,
        concat_axis=0,
        tiled=True,
    )
    returned = returned.reshape((-1,) + kv_pool.shape[1:])
    owner_pick = (
        entries.reshape(-1)[:, None] == jnp.arange(kv_pool.shape[0], dtype=jnp.int32)[None, :]
    ).astype(jnp.bfloat16)
    pool_grads = jnp.einsum(
        "ep,ekjw->pkjw", owner_pick, returned, preferred_element_type=jnp.float32
    )
    return (context, grad_queries, pool_grads.astype(jnp.bfloat16))


def solution(mesh):
    in_specs = (
        P("enc", "seq", None),
        P("enc", None, None, "seq"),
        P("enc", None, None),
        P("enc", None, None),
        P("enc", "seq", None),
    )
    out_specs = (P("enc", "seq", None), P("enc", "seq", None), P("enc", None, None, "seq"))
    return jax.shard_map(local, mesh=mesh, in_specs=in_specs, out_specs=out_specs, check_vma=False)
```

profile of v0, /device:TPU:1, one launch (start us, length us, event | category | flops | bytes accessed | tf_op | source)
XLA Modules:
  0.0 602.9 jit_solution(16944894643721143449)
XLA Ops:
  0.6 9.6 %copy.57 = bf16[1,128,8192]{1,0,2:T(2,128)(2,1)} copy(bf16[1,128,8192]{2,1,0:T(8,128)(2,1)} %param.5) | data formatting | bytes 4194304 | tf_op args[0]
  10.8 46.5 %reduce = bf16[8192,128]{1,0:T(8,128)(2,1)} reduce(bf16[8192,1,128]{2,1,0:T(2,128)(2,1)} %bitcast.134, bf16[]{:T(256)} %broadcast.101), dimensions={1}, to_apply=%bitcast.102.reduce_sub_computation | reduce | bytes 4194306
  61.2 7.6 %all-to-all-start = ((bf16[16,2,32768]{2,1,0:T(2,128)(2,1)}), bf16[16,2,32768]{2,1,0:T(2,128)(2,1)}, u32[]{:S(2)}, u32[]{:S(2)}) async-start(bf16[16,2,32768]{2,1,0:T(2,128)(2,1)} %reshape.129), calls=%async_computation | async-start | bytes 4194304 | tf_op jit(solution)/shard_map/all_to_all | solution.py:12
  68.9 9.5 %copy.66 = bf16[1,128,8192]{1,0,2:T(2,128)(2,1)} copy(bf16[1,128,8192]{2,1,0:T(8,128)(2,1)} %param.9) | data formatting | bytes 4194304 | tf_op args[4]
  78.3 46.5 %reduce.2 = bf16[8192,128]{1,0:T(8,128)(2,1)} reduce(bf16[8192,1,128]{2,1,0:T(2,128)(2,1)} %bitcast.141, bf16[]{:T(256)} %broadcast.101), dimensions={1}, to_apply=%bitcast.106.reduce_sub_computation | reduce | bytes 4194306
  128.8 6.7 %all-to-all-start.3 = ((bf16[16,2,32768]{2,1,0:T(2,128)(2,1)}), bf16[16,2,32768]{2,1,0:T(2,128)(2,1)}, u32[]{:S(2)}, u32[]{:S(2)}) async-start(bf16[16,2,32768]{2,1,0:T(2,128)(2,1)} %reshape.133), calls=%async_computation.3 | async-start | bytes 4194304 | tf_op jit(solution)/shard_map/all_to_all | solution.py:12
  138.3 26.0 %all-to-all-done.3 = bf16[16,2,32768]{2,1,0:T(2,128)(2,1)} async-done(((bf16[16,2,32768]{2,1,0:T(2,128)(2,1)}), bf16[16,2,32768]{2,1,0:T(2,128)(2,1)}, u32[]{:S(2)}, u32[]{:S(2)}) %all-to-all-start.3) | async-done | bytes 2097184 | tf_op jit(solution)/shard_map/all_to_all | solution.py:12
  164.2 11.7 %all-to-all-start.1 = ((bf16[16,1,2,128,512]{4,3,2,1,0:T(8,128)(2,1)}), bf16[16,1,2,128,512]{4,3,2,1,0:T(8,128)(2,1)}, u32[]{:S(2)}, u32[]{:S(2)}) async-start(bf16[16,1,2,128,512]{4,3,2,1,0:T(8,128)(2,1)} %bitcast.142), calls=%async_computation.1 | async-start | bytes 8388608 | tf_op jit(solution)/shard_map/all_to_all | solution.py:21
  175.9 10.5 %reshape.130 = bf16[8192,1,128]{2,1,0:T(2,128)(2,1)} reshape(bf16[16,2,32768]{2,1,0:T(2,128)(2,1)} %all-to-all-done) | data formatting | bytes 4194304
  197.5 10.5 %reshape.134 = bf16[8192,1,128]{2,1,0:T(2,128)(2,1)} reshape(bf16[16,2,32768]{2,1,0:T(2,128)(2,1)} %all-to-all-done.3) | data formatting | bytes 4194304
  223.1 46.4 %all-to-all-done.1 = bf16[16,1,2,128,512]{4,3,2,1,0:T(8,128)(2,1)} async-done(((bf16[16,1,2,128,512]{4,3,2,1,0:T(8,128)(2,1)}), bf16[16,1,2,128,512]{4,3,2,1,0:T(8,128)(2,1)}, u32[]{:S(2)}, u32[]{:S(2)}) %all-to-all-start.1) | async-done | bytes 4194336 | tf_op jit(solution)/shard_map/all_to_all | solution.py:21
  269.5 6.4 %copy.61 = bf16[16,1,2,128,512]{3,4,2,0,1:T(8,128)(2,1)} copy(bf16[16,1,2,128,512]{4,3,2,1,0:T(8,128)(2,1)} %all-to-all-done.1) | data formatting | bytes 8388608 | tf_op jit(solution)/shard_map/all_to_all | solution.py:21
  327.9 18.5 %copy.158 = bf16[1,2048,512]{2,0,1:T(2,128)(2,1)} copy(bf16[1,2048,512]{2,1,0:T(8,128)(2,1)S(1)} %pad_bitcast_fusion.1) | data formatting | bytes 4194304 | tf_op jit(solution)/shard_map/broadcast_in_dim | solution.py:86
  346.4 15.4 %reduce.1 = bf16[2048,512]{1,0:T(8,128)(2,1)} reduce(bf16[2048,1,512]{2,1,0:T(2,128)(2,1)} %bitcast.138, bf16[]{:T(256)} %broadcast.101), dimensions={1}, to_apply=%bitcast.133.reduce_sub_computation | reduce | bytes 4194306
  376.9 8.0 %multiply_reduce_fusion = (f32[32,4,64]{2,1,0:T(4,128)S(1)}, f32[32,4,64]{2,1,0:T(4,128)S(1)}, f32[32,4,64,128]{3,2,1,0:T(8,128)}) fusion(f32[32,4,64]{2,1,0:T(4,128)S(1)} %add.65, f32[32,4,64]{2,1,0:T(4,128)S(1)} %max.8, f32[32,4,64,128]{3,2,1,0:T(8,128)S(1)} %copy-done.5, f32[32,4,64,128]{3,2,1,0:T(8,128)S(1)} %fusion.23, ...), kind=kOutput, calls=%fused_computation.22 | convolution fusion | flops 278904832 | bytes 23199744 | tf_op jit(solution)/shard_map/chid,chjd->chij/dot_general | solution.py:90
  399.1 18.9 %copy.157 = bf16[1,2048,512]{2,0,1:T(2,128)(2,1)} copy(bf16[1,2048,512]{2,1,0:T(8,128)(2,1)S(1)} %pad_bitcast_fusion) | data formatting | bytes 4194304 | tf_op jit(solution)/shard_map/broadcast_in_dim | solution.py:106
  418.1 15.4 %reduce.3 = bf16[2048,512]{1,0:T(8,128)(2,1)} reduce(bf16[2048,1,512]{2,1,0:T(2,128)(2,1)} %bitcast.135, bf16[]{:T(256)} %broadcast.101), dimensions={1}, to_apply=%bitcast.132.reduce_sub_computation | reduce | bytes 4194306
  457.3 7.1 %all-to-all-start.4 = ((bf16[16,2,32768]{2,1,0:T(2,128)(2,1)}), bf16[16,2,32768]{2,1,0:T(2,128)(2,1)}, u32[]{:S(2)}, u32[]{:S(2)}) async-start(bf16[16,2,32768]{2,1,0:T(2,128)(2,1)} %reshape.135), calls=%async_computation.4 | async-start | bytes 4194304 | tf_op jit(solution)/shard_map/all_to_all | solution.py:16
  464.4 6.8 %convolution_convert_fusion.1 = bf16[32,4,128,128]{3,2,1,0:T(8,128)(2,1)S(1)} fusion(bf16[32,64,4,128]{3,2,1,0:T(4,128)(2,1)S(1)} %copy-done.18, f32[32,4,64,128]{3,2,1,0:T(8,128)} %copy-done.2, f32[32,4,64]{2,1,0:T(4,128)S(1)} %add.65, f32[32,4,64]{2,1,0:T(4,128)S(1)} %max.8), kind=kOutput, calls=%fused_computation.34 | convolution fusion | flops 274726912 | bytes 10551296 | tf_op jit(solution)/shard_map/chij,chid->chjd/dot_general | solution.py:115
  479.6 7.5 %copy.76 = bf16[16,2,128,4,128]{2,4,3,1,0:T(8,128)(2,1)} copy(bf16[16,2,128,4,128]{4,0,2,3,1:T(8,128)(2,1)} %maximum_bitcast_fusion) | data formatting | bytes 8388608 | tf_op jit(solution)/shard_map/transpose | solution.py:125
  493.5 8.9 %all-to-all-start.5 = ((bf16[16,1,2,128,512]{4,3,2,1,0:T(8,128)(2,1)}), bf16[16,1,2,128,512]{4,3,2,1,0:T(8,128)(2,1)}, u32[]{:S(2)}, u32[]{:S(2)}) async-start(bf16[16,1,2,128,512]{4,3,2,1,0:T(8,128)(2,1)} %copy.77), calls=%async_computation.5 | async-start | bytes 8388608 | tf_op jit(solution)/shard_map/all_to_all | solution.py:126
  502.4 10.5 %reshape.132 = bf16[2048,1,512]{2,1,0:T(2,128)(2,1)} reshape(bf16[16,2,32768]{2,1,0:T(2,128)(2,1)} %all-to-all-done.2) | data formatting | bytes 4194304
  522.1 10.5 %reshape.136 = bf16[2048,1,512]{2,1,0:T(2,128)(2,1)} reshape(bf16[16,2,32768]{2,1,0:T(2,128)(2,1)} %all-to-all-done.4) | data formatting | bytes 4194304
  541.8 54.0 %all-to-all-done.5 = bf16[16,1,2,128,512]{4,3,2,1,0:T(8,128)(2,1)} async-done(((bf16[16,1,2,128,512]{4,3,2,1,0:T(8,128)(2,1)}), bf16[16,1,2,128,512]{4,3,2,1,0:T(8,128)(2,1)}, u32[]{:S(2)}, u32[]{:S(2)}) %all-to-all-start.5) | async-done | bytes 4194336 | tf_op jit(solution)/shard_map/all_to_all | solution.py:126
  (113 shorter events, 182.5 us)
Async XLA Ops:
  0.6 134.8 %copy-start = (bf16[8,2,128,512]{3,2,1,0:T(8,128)(2,1)S(1)}, bf16[8,2,128,512]{3,2,1,0:T(8,128)(2,1)}, u32[]{:S(2)}) copy-start(bf16[8,2,128,512]{3,2,1,0:T(8,128)(2,1)} %param.6) | copy-start | bytes 6291460
  61.2 67.5 %all-to-all-start = ((bf16[16,2,32768]{2,1,0:T(2,128)(2,1)}), bf16[16,2,32768]{2,1,0:T(2,128)(2,1)}, u32[]{:S(2)}, u32[]{:S(2)}) async-start(bf16[16,2,32768]{2,1,0:T(2,128)(2,1)} %reshape.129), calls=%async_computation | async-start | bytes 4194304 | tf_op jit(solution)/shard_map/all_to_all | solution.py:12
  124.8 10.6 %copy-start.21 = (s32[1,16,1]{1,2,0:T(1,128)S(1)}, s32[1,16,1]{1,2,0:T(1,128)}, u32[]{:S(2)}) copy-start(s32[1,16,1]{1,2,0:T(1,128)} %param.7) | copy-start | bytes 196
  128.8 35.5 %all-to-all-start.3 = ((bf16[16,2,32768]{2,1,0:T(2,128)(2,1)}), bf16[16,2,32768]{2,1,0:T(2,128)(2,1)}, u32[]{:S(2)}, u32[]{:S(2)}) async-start(bf16[16,2,32768]{2,1,0:T(2,128)(2,1)} %reshape.133), calls=%async_computation.3 | async-start | bytes 4194304 | tf_op jit(solution)/shard_map/all_to_all | solution.py:12
  164.2 11.7 %copy-start.20 = (s32[1,32,2]{1,2,0:T(2,128)S(1)}, s32[1,32,2]{1,2,0:T(2,128)}, u32[]{:S(2)}) copy-start(s32[1,32,2]{1,2,0:T(2,128)} %param.8) | copy-start | bytes 772
  164.2 105.3 %all-to-all-start.1 = ((bf16[16,1,2,128,512]{4,3,2,1,0:T(8,128)(2,1)}), bf16[16,1,2,128,512]{4,3,2,1,0:T(8,128)(2,1)}, u32[]{:S(2)}, u32[]{:S(2)}) async-start(bf16[16,1,2,128,512]{4,3,2,1,0:T(8,128)(2,1)} %bitcast.142), calls=%async_computation.1 | async-start | bytes 8388608 | tf_op jit(solution)/shard_map/all_to_all | solution.py:21
  305.4 5.4 copy-start.7
  310.8 7.0 %copy-start.2 = (f32[32,4,64,128]{3,2,1,0:T(8,128)}, f32[32,4,64,128]{3,2,1,0:T(8,128)S(1)}, u32[]{:S(2)}) copy-start(f32[32,4,64,128]{3,2,1,0:T(8,128)S(1)} %get-tuple-element.31) | copy-start | bytes 12582916
  314.0 7.8 %copy-start.4 = (f32[32,4,64,128]{3,2,1,0:T(8,128)}, f32[32,4,64,128]{3,2,1,0:T(8,128)S(1)}, u32[]{:S(2)}) copy-start(f32[32,4,64,128]{3,2,1,0:T(8,128)S(1)} %get-tuple-element.33) | copy-start | bytes 12582916
  317.9 4.0 copy-start.19
  366.2 91.1 %all-to-all-start.2 = ((bf16[16,2,32768]{2,1,0:T(2,128)(2,1)}), bf16[16,2,32768]{2,1,0:T(2,128)(2,1)}, u32[]{:S(2)}, u32[]{:S(2)}) async-start(bf16[16,2,32768]{2,1,0:T(2,128)(2,1)} %reshape.131), calls=%async_computation.2 | async-start | bytes 4194304 | tf_op jit(solution)/shard_map/all_to_all | solution.py:16
  370.9 6.0 copy-start.3
  370.9 6.0 copy-start.5
  370.9 6.0 copy-start.16
  385.0 5.4 copy-start.9
  437.9 5.0 copy-start.6
  437.9 5.0 copy-start.17
  448.5 4.4 copy-start.13
  457.3 7.1 %copy-start.18 = (bf16[32,64,4,128]{3,2,1,0:T(4,128)(2,1)S(1)}, bf16[32,64,4,128]{3,2,1,0:T(4,128)(2,1)}, u32[]{:S(2)}) copy-start(bf16[32,64,4,128]{3,2,1,0:T(4,128)(2,1)} %reshape.83) | copy-start | bytes 6291460
  457.3 36.2 %all-to-all-start.4 = ((bf16[16,2,32768]{2,1,0:T(2,128)(2,1)}), bf16[16,2,32768]{2,1,0:T(2,128)(2,1)}, u32[]{:S(2)}, u32[]{:S(2)}) async-start(bf16[16,2,32768]{2,1,0:T(2,128)(2,1)} %reshape.135), calls=%async_computation.4 | async-start | bytes 4194304 | tf_op jit(solution)/shard_map/all_to_all | solution.py:16
  464.4 6.8 %copy-start.15 = (f32[16,4,128,128]{3,0,2,1:T(8,128)S(1)}, f32[16,4,128,128]{3,0,2,1:T(8,128)}, u32[]{:S(2)}) copy-start(f32[16,4,128,128]{3,0,2,1:T(8,128)} %fusion.3) | copy-start | bytes 12582916
  493.5 102.3 %all-to-all-start.5 = ((bf16[16,1,2,128,512]{4,3,2,1,0:T(8,128)(2,1)}), bf16[16,1,2,128,512]{4,3,2,1,0:T(8,128)(2,1)}, u32[]{:S(2)}, u32[]{:S(2)}) async-start(bf16[16,1,2,128,512]{4,3,2,1,0:T(8,128)(2,1)} %copy.77), calls=%async_computation.5 | async-start | bytes 8388608 | tf_op jit(solution)/shard_map/all_to_all | solution.py:126
  535.4 60.5 %copy-start.22 = (s32[1,16,1]{1,2,0:T(1,128)S(1)}, s32[1,16,1]{1,2,0:T(1,128)}, u32[]{:S(2)}) copy-start(s32[1,16,1]{1,2,0:T(1,128)} %param.7) | copy-start | bytes 196
  595.9 6.8 %copy-start.1 = (bf16[8,2,128,512]{3,2,1,0:T(8,128)(2,1)S(1)}, bf16[8,2,128,512]{3,2,1,0:T(8,128)(2,1)}, u32[]{:S(2)}) copy-start(bf16[8,2,128,512]{3,2,1,0:T(8,128)(2,1)} %param.6) | copy-start | bytes 6291460
  (5 other events, 14.6 us)
where the time goes:
time: 615 us; the launch traced here: 603 us
  local copies, waits for them, and re-layouts  222 us (36%)
  other arithmetic  135 us (22%)
  waiting for transfers between devices  126 us (20%)
  matrix products  71.4 us (12%)
  starting transfers between devices  46.5 us (8%)
    unnamed x4, other arithmetic  124 us
    unnamed x66, local copies, waits for them, and re-layouts  102 us
    all_to_all x1, waiting for transfers between devices, local(): lax.all_to_all(slot_grads.reshape(entries.shape + slot_grads.shape[1:]),...  54 us
    all_to_all x1, waiting for transfers between devices, fetch_slots(): lax.all_to_all(outgoing, 'enc', split_axis=0, concat_axis=0, tiled=True)  46.4 us
    all_to_all x2, waiting for transfers between devices, to_heads(): lax.all_to_all(token_major, 'seq', split_axis=2, concat_axis=1, tiled=True)  26 us
    broadcast_in_dim x2, local copies, waits for them, and re-layouts, local(): out_of_blocks(query_grads.astype(jnp.bfloat16))[None]  19.4 us
    broadcast_in_dim x2, local copies, waits for them, and re-layouts, local(): context = to_tokens(out_of_blocks(out_blocks.astype(jnp.bfloat16))[None])  19 us
    all_to_all x2, starting transfers between devices, to_heads(): lax.all_to_all(token_major, 'seq', split_axis=2, concat_axis=1, tiled=True)  14.3 us
  transfers between devices with their start and end apart: 6, of which 3 were waited for; matrix products, arithmetic and copies ran while one was open for 44% of the time, Pallas kernels for 0%

commit v1 on v0

v1 whole, which is shorter than its diff:
```python
import functools

import jax
import jax.numpy as jnp
from jax import lax
from jax.experimental import pallas as pl
from jax.experimental.pallas import tpu as pltpu
from jax.sharding import PartitionSpec as P

DH = 128
BLOCK = 64
NBLEN = 128
MESH = pl.DeviceIdType.MESH
ANY = pl.BlockSpec(memory_space=pl.ANY)
SCALAR = pl.BlockSpec(memory_space=pltpu.SMEM)
MIB = 1 << 20


def greet(enc_count, seq_count, enc_here, seq_here):
    barrier = pltpu.get_barrier_semaphore()
    for k in range(1, enc_count):
        peer = lax.rem(enc_here + k, enc_count)
        pl.semaphore_signal(barrier, inc=1, device_id={"enc": peer}, device_id_type=MESH)
    for k in range(1, seq_count):
        peer = lax.rem(seq_here + k, seq_count)
        pl.semaphore_signal(barrier, inc=1, device_id={"seq": peer}, device_id_type=MESH)
    return barrier


def remote(source, target, sems, which, axis, peer):
    return pltpu.make_async_remote_copy(
        src_ref=source,
        dst_ref=target,
        send_sem=sems.at[0, which],
        recv_sem=sems.at[1, which],
        device_id={axis: peer},
        device_id_type=MESH,
    )


def gather_kernel(
    enc_count, seq_count, entries, queries, grads, pool, head_queries, head_grads, arrived,
    outgoing, enc_sems, query_sems, grad_sems, own_sems,
):
    enc_here, seq_here = lax.axis_index("enc"), lax.axis_index("seq")
    rows, width = queries.shape[0], pool.shape[-1]
    barrier = greet(enc_count, seq_count, enc_here, seq_here)

    def pick(e, carry):
        outgoing[e] = pool[entries[e]]
        return carry

    lax.fori_loop(0, enc_count, pick, 0)
    pl.semaphore_wait(barrier, enc_count + seq_count - 2)

    copies = []
    far = enc_count // 2
    for k in sorted(range(1, enc_count), key=lambda k: -min(k, enc_count - k)):
        peer = lax.rem(enc_here + k, enc_count)
        copies.append(remote(outgoing.at[peer], arrived.at[enc_here], enc_sems, k, "enc", peer))
        copies[-1].start()
    mine = pl.ds(pl.multiple_of(seq_here * rows, rows), rows)
    for source, target, sems in ((queries, head_queries, query_sems), (grads, head_grads, grad_sems)):
        for k in range(1, seq_count):
            peer = lax.rem(seq_here + k, seq_count)
            part = pl.ds(pl.multiple_of(peer * width, width), width)
            copies.append(remote(source.at[:, part], target.at[mine, :], sems, k, "seq", peer))
            copies[-1].start()
    part = pl.ds(pl.multiple_of(seq_here * width, width), width)
    for n, (source, target) in enumerate((
        (outgoing.at[enc_here], arrived.at[enc_here]),
        (queries.at[:, part], head_queries.at[mine, :]),
        (grads.at[:, part], head_grads.at[mine, :]),
    )):
        copies.append(pltpu.make_async_copy(source, target, own_sems.at[n]))
        copies[-1].start()
    for copy in copies:
        copy.wait()


def gather(enc_count, seq_count, entries, queries, grads, pool):
    rows, width = queries.shape[0], pool.shape[-1]
    heads = jax.ShapeDtypeStruct((rows * seq_count, width), queries.dtype)
    received = (enc_count,) + pool.shape[1:]
    return pl.pallas_call(
        functools.partial(gather_kernel, enc_count, seq_count),
        out_shape=(heads, heads, jax.ShapeDtypeStruct(received, pool.dtype)),
        in_specs=[SCALAR, ANY, ANY, pl.BlockSpec(memory_space=pltpu.VMEM)],
        out_specs=(ANY, ANY, ANY),
        scratch_shapes=[
            pltpu.VMEM(received, pool.dtype),
            pltpu.SemaphoreType.DMA((2, enc_count)),
            pltpu.SemaphoreType.DMA((2, seq_count)),
            pltpu.SemaphoreType.DMA((2, seq_count)),
            pltpu.SemaphoreType.DMA((3,)),
        ],
        compiler_params=pltpu.CompilerParams(
            collective_id=0, has_side_effects=True, vmem_limit_bytes=24 * MIB
        ),
    )(entries, queries, grads, pool)


def attend_kernel(slots, queries, grads, received, context, grad_queries, slot_grads, total):
    blocks = queries.shape[0] // BLOCK
    scale = DH ** (-0.5)
    total[...] = jnp.zeros_like(total)
    is_last = lax.broadcasted_iota(jnp.int32, (BLOCK, 2 * DH), 0) == BLOCK - 1
    is_first_head = lax.broadcasted_iota(jnp.int32, (BLOCK, 2 * DH), 1) < DH
    nt = (((1,), (1,)), ((), ()))
    tn = (((0,), (0,)), ((), ()))
    f32 = jnp.float32

    def moved(ref, b):
        here = ref[pl.ds(pl.multiple_of(b * BLOCK, BLOCK), BLOCK), :].astype(f32)
        after = jnp.minimum(b + 1, blocks - 1)
        later = ref[pl.ds(pl.multiple_of(after * BLOCK, BLOCK), BLOCK), :].astype(f32)
        later = jnp.where(b + 1 < blocks, later, 0.0)
        row = jnp.where(is_last, here, later)
        pair = [jnp.where(is_first_head, row, 0.0), jnp.where(is_first_head, 0.0, row)]
        return jnp.concatenate(pair, axis=0).astype(jnp.bfloat16)

    def both(wide):
        return jnp.where(is_first_head, wide[:BLOCK], wide[BLOCK:])

    def step(b, carry):
        last_out, last_grad = carry
        first, second = slots[2 * b], slots[2 * b + 1]
        query, grad = moved(queries, b), moved(grads, b)
        keys = jnp.concatenate([received[first, 0], received[second, 0]], axis=0)
        values = jnp.concatenate([received[first, 1], received[second, 1]], axis=0)
        scores = lax.dot_general(query, keys, nt, preferred_element_type=f32) * scale
        weights = jnp.exp(scores - jnp.max(scores, axis=-1, keepdims=True))
        probs = weights * (1.0 / jnp.sum(weights, axis=-1, keepdims=True))
        probs_low = probs.astype(jnp.bfloat16)
        out = both(jnp.dot(probs_low, values, preferred_element_type=f32))
        grad_probs = lax.dot_general(grad, values, nt, preferred_element_type=f32)
        inner = jnp.sum(probs * grad_probs, axis=-1, keepdims=True)
        grad_scores = (probs * (grad_probs - inner) * scale).astype(jnp.bfloat16)
        query_grad = both(jnp.dot(grad_scores, keys, preferred_element_type=f32))
        key_grad = lax.dot_general(grad_scores, query, tn, preferred_element_type=f32)
        value_grad = lax.dot_general(probs_low, grad, tn, preferred_element_type=f32)
        total[first, 0] += key_grad[:NBLEN]
        total[first, 1] += value_grad[:NBLEN]
        total[second, 0] += key_grad[NBLEN:]
        total[second, 1] += value_grad[NBLEN:]
        here = pl.ds(pl.multiple_of(b * BLOCK, BLOCK), BLOCK)
        context[here, :] = jnp.where(is_last, out, last_out).astype(context.dtype)
        grad_queries[here, :] = jnp.where(is_last, query_grad, last_grad).astype(context.dtype)
        return out, query_grad

    zeros = jnp.zeros((BLOCK, 2 * DH), f32)
    lax.fori_loop(0, blocks, step, (zeros, zeros), unroll=2)
    slot_grads[...] = total[...].astype(slot_grads.dtype)


def attend(slots, head_queries, head_grads, received):
    length, width = head_queries.shape
    entries = received.shape[0]
    pair = 2 * DH
    rows = pl.BlockSpec((length, pair), lambda h: (0, h))
    pool = pl.BlockSpec((entries, 2, NBLEN, pair), lambda h: (0, 0, 0, h))
    return pl.pallas_call(
        attend_kernel,
        out_shape=(
            jax.ShapeDtypeStruct(head_queries.shape, head_queries.dtype),
            jax.ShapeDtypeStruct(head_queries.shape, head_queries.dtype),
            jax.ShapeDtypeStruct(received.shape, received.dtype),
        ),
        grid=(width // pair,),
        in_specs=[SCALAR, rows, rows, pool],
        out_specs=(rows, rows, pool),
        scratch_shapes=[pltpu.VMEM((entries, 2, NBLEN, pair), jnp.float32)],
        compiler_params=pltpu.CompilerParams(vmem_limit_bytes=40 * MIB),
    )(slots, head_queries, head_grads, received)


def scatter_kernel(
    enc_count, seq_count, head_context, head_grads, slot_grads, context, grad_queries, returned,
    enc_sems, context_sems, grad_sems, own_sems,
):
    enc_here, seq_here = lax.axis_index("enc"), lax.axis_index("seq")
    rows, width = context.shape[0], head_context.shape[1]
    barrier = greet(enc_count, seq_count, enc_here, seq_here)
    pl.semaphore_wait(barrier, enc_count + seq_count - 2)
    copies = []
    for k in sorted(range(1, enc_count), key=lambda k: -min(k, enc_count - k)):
        peer = lax.rem(enc_here + k, enc_count)
        copies.append(remote(slot_grads.at[peer], returned.at[enc_here], enc_sems, k, "enc", peer))
        copies[-1].start()
    part = pl.ds(pl.multiple_of(seq_here * width, width), width)
    for source, target, sems in ((head_context, context, context_sems), (head_grads, grad_queries, grad_sems)):
        for k in range(1, seq_count):
            peer = lax.rem(seq_here + k, seq_count)
            theirs = pl.ds(pl.multiple_of(peer * rows, rows), rows)
            copies.append(remote(source.at[theirs, :], target.at[:, part], sems, k, "seq", peer))
            copies[-1].start()
    mine = pl.ds(pl.multiple_of(seq_here * rows, rows), rows)
    for n, (source, target) in enumerate((
        (slot_grads.at[enc_here], returned.at[enc_here]),
        (head_context.at[mine, :], context.at[:, part]),
        (head_grads.at[mine, :], grad_queries.at[:, part]),
    )):
        copies.append(pltpu.make_async_copy(source, target, own_sems.at[n]))
        copies[-1].start()
    for copy in copies:
        copy.wait()


def scatter(enc_count, seq_count, head_context, head_grads, slot_grads):
    length, width = head_context.shape
    tokens = jax.ShapeDtypeStruct((length // seq_count, width * seq_count), head_context.dtype)
    return pl.pallas_call(
        functools.partial(scatter_kernel, enc_count, seq_count),
        out_shape=(tokens, tokens, jax.ShapeDtypeStruct(slot_grads.shape, slot_grads.dtype)),
        in_specs=[ANY] * 3,
        out_specs=(ANY, ANY, ANY),
        scratch_shapes=[
            pltpu.SemaphoreType.DMA((2, enc_count)),
            pltpu.SemaphoreType.DMA((2, seq_count)),
            pltpu.SemaphoreType.DMA((2, seq_count)),
            pltpu.SemaphoreType.DMA((3,)),
        ],
        compiler_params=pltpu.CompilerParams(
            collective_id=1, has_side_effects=True, vmem_limit_bytes=4 * MIB
        ),
    )(head_context, head_grads, slot_grads)


def owner_kernel(entries, returned, context, grad_queries, pool_grads, context_out, grad_out, total, sems):
    moves = [
        pltpu.make_async_copy(context, context_out, sems.at[0]),
        pltpu.make_async_copy(grad_queries, grad_out, sems.at[1]),
    ]

    @pl.when(pl.program_id(0) == 0)
    def _():
        for move in moves:
            move.start()

    total[...] = jnp.zeros_like(total)

    def step(e, carry):
        total[entries[e]] += returned[e].astype(jnp.float32)
        return carry

    lax.fori_loop(0, returned.shape[0], step, 0)
    pool_grads[...] = total[...].astype(pool_grads.dtype)

    @pl.when(pl.program_id(0) == pl.num_programs(0) - 1)
    def _():
        for move in moves:
            move.wait()


def owner_sum(entries, returned, context, grad_queries, pool_shape):
    cuts = 4
    count, two, length, width = returned.shape
    part = length // cuts
    tokens = jax.ShapeDtypeStruct(context.shape, context.dtype)
    return pl.pallas_call(
        owner_kernel,
        out_shape=(jax.ShapeDtypeStruct(pool_shape, returned.dtype), tokens, tokens),
        grid=(cuts,),
        in_specs=[
            SCALAR,
            pl.BlockSpec((count, two, part, width), lambda i: (0, 0, i, 0)),
            ANY,
            ANY,
        ],
        out_specs=(pl.BlockSpec((pool_shape[0], two, part, width), lambda i: (0, 0, i, 0)), ANY, ANY),
        scratch_shapes=[
            pltpu.VMEM((pool_shape[0], two, part, width), jnp.float32),
            pltpu.SemaphoreType.DMA((2,)),
        ],
        compiler_params=pltpu.CompilerParams(vmem_limit_bytes=24 * MIB),
    )(entries, returned, context, grad_queries)


def local(enc_count, seq_count, queries, kv_pool, send_lists, block_slots, grad_context):
    entries = send_lists.reshape(-1)
    slots = block_slots.reshape(-1)
    head_queries, head_grads, received = gather(
        enc_count, seq_count, entries, queries[0], grad_context[0], kv_pool
    )
    head_context, head_query_grads, slot_grads = attend(slots, head_queries, head_grads, received)
    context, grad_queries, returned = scatter(
        enc_count, seq_count, head_context, head_query_grads, slot_grads
    )
    pool_grads, context, grad_queries = owner_sum(
        entries, returned, context, grad_queries, kv_pool.shape
    )
    return context[None], grad_queries[None], pool_grads


def solution(mesh):
    in_specs = (
        P("enc", "seq", None),
        P("enc", None, None, "seq"),
        P("enc", None, None),
        P("enc", None, None),
        P("enc", "seq", None),
    )
    out_specs = (P("enc", "seq", None), P("enc", "seq", None), P("enc", None, None, "seq"))
    body = functools.partial(local, mesh.shape["enc"], mesh.shape["seq"])
    return jax.shard_map(body, mesh=mesh, in_specs=in_specs, out_specs=out_specs, check_vma=False)
```

time: 615 us -> 264 us (0.43); the launches traced: 603 us -> 264 us
  Pallas kernels: 0 us -> 255 us
  local copies, waits for them, and re-layouts: 222 us -> 8.23 us
  other arithmetic: 135 us -> 0 us
  waiting for transfers between devices: 126 us -> 0 us
  matrix products: 71.4 us -> 0 us
  starting transfers between devices: 46.5 us -> 0 us
    pallas_call x0 -> x4, Pallas kernels: none -> 255 us  [the longest x1 102 us: gather(): pl.pallas_call(functools.partial(gather_kernel, enc_count, seq_count), ou...]
    all_to_all x6 -> x0, waiting for transfers between devices: 126 us -> none  [the longest x1 54 us: local(): lax.all_to_all(slot_grads.reshape(entries.shape + slot_grads.shape[1:]),...]
    unnamed x4 -> x0, other arithmetic: 124 us -> none
    unnamed x66 -> x13, local copies, waits for them, and re-layouts: 102 us -> 8.13 us
    dot_general x17 -> x0, matrix products: 71.4 us -> none  [the longest x2 14 us: local(): jnp.einsum('chid,chjd->chij', grads_moved, values, preferred_element_type...]
    all_to_all x6 -> x0, starting transfers between devices: 46.5 us -> none  [the longest x2 14.3 us: to_heads(): lax.all_to_all(token_major, 'seq', split_axis=2, concat_axis=1, tiled=True)]
    broadcast_in_dim x4 -> x0, local copies, waits for them, and re-layouts: 38.4 us -> none  [the longest x2 19.4 us: local(): out_of_blocks(query_grads.astype(jnp.bfloat16))[None]]
    gather x5 -> x0, local copies, waits for them, and re-layouts: 21.3 us -> none  [the longest x1 4.65 us: forward_parts(): pool_heads[:, 1][block_use[:, 1]]]
  transfers between devices with their start and end apart: 6 -> 0, of which waited for: 3 -> 0; matrix products, arithmetic and copies ran while one was open for 44% -> 0% of each run, Pallas kernels for 0% -> 0%
where the time goes in v1:
time: 264 us
  Pallas kernels  255 us (97%)
  local copies, waits for them, and re-layouts  8.23 us (3%)
    pallas_call x1, Pallas kernels, gather(): pl.pallas_call(functools.partial(gather_kernel, enc_count, seq_count), ou...  102 us
    pallas_call x1, Pallas kernels, scatter(): pl.pallas_call(functools.partial(scatter_kernel, enc_count, seq_count), o...  98.6 us
    pallas_call x1, Pallas kernels, attend(): pl.pallas_call(attend_kernel, out_shape=(jax.ShapeDtypeStruct(head_querie...  50.2 us
    unnamed x13, local copies, waits for them, and re-layouts  8.13 us

profile of v1, /device:TPU:1, one launch (start us, length us, event | category | flops | bytes accessed | tf_op | source)
XLA Modules:
  0.0 264.1 jit_solution(8637982489217187705)
XLA Ops:
  0.6 0.8 copy.9
  1.4 0.1 reshape.13.slots
  1.5 0.0 copy-start.1
  1.5 1.6 copy-done.1
  3.1 0.0 copy-start.2
  3.1 1.6 copy-done.2
  4.7 0.0 copy-start.3
  4.7 1.6 copy-done.3
  6.3 0.0 copy-start.4
  6.3 0.7 copy-done.4
  6.9 101.9 %shard_map.76 = (bf16[2048,512]{1,0:T(8,128)(2,1)S(1)}, bf16[2048,512]{1,0:T(8,128)(2,1)S(1)}, bf16[16,2,128,512]{3,2,1,0:T(8,128)(2,1)S(1)}) custom-call(s32[16]{0:T(128)S(1)} %bitcast.7, bf16[128,8192]{1,0:T(8,128)(2,1)S(1)} %bitcast.5, bf16[128,8192]{1,0:T(8,128)(2,1)S(1)} %bitcast.6, bf16[8,2,128,512]{3,2,1,0:T(8,128)(2,1)S(1)} %copy-done.3), custom_call_target="tpu_custom_call" | custom-call | tf_op jit(solution)/shard_map/pallas_call | solution.py:85
  108.8 0.0 copy-start
  108.8 1.9 copy-done
  110.7 50.2 %shard_map.77 = (bf16[2048,512]{1,0:T(8,128)(2,1)S(1)}, bf16[2048,512]{1,0:T(8,128)(2,1)S(1)}, bf16[16,2,128,512]{3,2,1,0:T(8,128)(2,1)S(1)}) custom-call(s32[64]{0:T(128)S(1)} %reshape.13.slots, bf16[2048,512]{1,0:T(8,128)(2,1)S(1)} %get-tuple-element.15.queries, bf16[2048,512]{1,0:T(8,128)(2,1)S(1)} %get-tuple-element.16.grads, ...), custom_call_target="tpu_custom_call" | custom-call | tf_op jit(solution)/shard_map/pallas_call | solution.py:162
  161.0 0.0 copy-start.5
  161.0 98.6 %shard_map.78 = (bf16[128,8192]{1,0:T(8,128)(2,1)S(1)}, bf16[128,8192]{1,0:T(8,128)(2,1)S(1)}, bf16[16,2,128,512]{3,2,1,0:T(8,128)(2,1)S(1)}) custom-call(bf16[2048,512]{1,0:T(8,128)(2,1)S(1)} %get-tuple-element.18.head_context, bf16[2048,512]{1,0:T(8,128)(2,1)S(1)} %get-tuple-element.19.head_grads, bf16[16,2,128,512]{3,2,1,0:T(8,128)(2,1)S(1)} %get-tuple-element.20.slot_grads), custom_call_target="tpu_custom_call" | custom-call | tf_op jit(solution)/shard_map/pallas_call | solution.py:212
  259.6 0.0 copy-done.5
  259.6 4.4 %shard_map.79 = (bf16[8,2,128,512]{3,2,1,0:T(8,128)(2,1)}, bf16[128,8192]{1,0:T(8,128)(2,1)}, bf16[128,8192]{1,0:T(8,128)(2,1)}) custom-call(s32[16]{0:T(128)S(1)} %bitcast.8, bf16[16,2,128,512]{3,2,1,0:T(8,128)(2,1)S(1)} %get-tuple-element.21.returned, bf16[128,8192]{1,0:T(8,128)(2,1)S(1)} %get-tuple-element.22.context, ...), custom_call_target="tpu_custom_call" | custom-call | tf_op jit(solution)/shard_map/pallas_call | solution.py:260
Async XLA Ops:
  1.5 1.6 copy-start.1
  3.1 1.6 copy-start.2
  4.7 1.6 copy-start.3
  6.3 0.7 copy-start.4
  108.8 1.9 copy-start
  161.0 98.6 %copy-start.5 = (s32[1,16,1]{1,2,0:T(1,128)S(1)}, s32[1,16,1]{1,2,0:T(1,128)}, u32[]{:S(2)}) copy-start(s32[1,16,1]{1,2,0:T(1,128)} %param.7) | copy-start | bytes 196

commit v2 on v1

v2 whole, which is shorter than its diff:
```python
import functools

import jax
import jax.numpy as jnp
from jax import lax
from jax.experimental import pallas as pl
from jax.experimental.pallas import tpu as pltpu
from jax.sharding import PartitionSpec as P

DH = 128
BLOCK = 64
NBLEN = 128
PAIR = 2 * DH
MESH = pl.DeviceIdType.MESH
ANY = pl.BlockSpec(memory_space=pl.ANY)
SCALAR = pl.BlockSpec(memory_space=pltpu.SMEM)
MIB = 1 << 20
NT = (((1,), (1,)), ((), ()))
TN = (((0,), (0,)), ((), ()))
F32 = jnp.float32
BF16 = jnp.bfloat16


def sort_kernel(slots, order, fresh, last, count):
    uses, entries = slots.shape[0], last.shape[0]

    def clear(s, carry):
        count[s] = 0
        return carry

    def tally(u, carry):
        count[slots[u]] += 1
        fresh[u] = 0
        return carry

    def starts(s, begin):
        size = count[s]
        count[s] = begin
        last[s] = begin + size - 1
        fresh[begin] = 1
        return begin + size

    def place(u, carry):
        slot = slots[u]
        order[count[slot]] = u
        count[slot] += 1
        return carry

    lax.fori_loop(0, entries, clear, 0)
    lax.fori_loop(0, uses, tally, 0)
    lax.fori_loop(0, entries, starts, 0)
    lax.fori_loop(0, uses, place, 0)


def sort_uses(slots, entries):
    uses = slots.shape[0]
    return pl.pallas_call(
        sort_kernel,
        out_shape=(
            jax.ShapeDtypeStruct((uses,), jnp.int32),
            jax.ShapeDtypeStruct((uses,), jnp.int32),
            jax.ShapeDtypeStruct((entries,), jnp.int32),
        ),
        in_specs=[SCALAR],
        out_specs=(SCALAR,) * 3,
        scratch_shapes=[pltpu.SMEM((entries,), jnp.int32)],
    )(slots)


def block_pass(slots, queries, grads, received, out, query_grads, wide_q, wide_g, probs_kept, scores_kept):
    blocks = queries.shape[0] // BLOCK
    scale = DH ** (-0.5)
    is_last = lax.broadcasted_iota(jnp.int32, (BLOCK, PAIR), 0) == BLOCK - 1
    is_first_head = lax.broadcasted_iota(jnp.int32, (BLOCK, PAIR), 1) < DH

    def moved(ref, b):
        here = ref[pl.ds(pl.multiple_of(b * BLOCK, BLOCK), BLOCK), :].astype(F32)
        after = jnp.minimum(b + 1, blocks - 1)
        later = ref[pl.ds(pl.multiple_of(after * BLOCK, BLOCK), BLOCK), :].astype(F32)
        later = jnp.where(b + 1 < blocks, later, 0.0)
        row = jnp.where(is_last, here, later)
        pair = [jnp.where(is_first_head, row, 0.0), jnp.where(is_first_head, 0.0, row)]
        return jnp.concatenate(pair, axis=0).astype(BF16)

    def both(wide):
        return jnp.where(is_first_head, wide[:BLOCK], wide[BLOCK:])

    def step(b, carry):
        last_out, last_grad = carry
        first, second = slots[2 * b], slots[2 * b + 1]
        query, grad = moved(queries, b), moved(grads, b)
        wide_q[b] = query
        wide_g[b] = grad
        keys = jnp.concatenate([received[first, 0], received[second, 0]], axis=0)
        values = jnp.concatenate([received[first, 1], received[second, 1]], axis=0)
        scores = lax.dot_general(query, keys, NT, preferred_element_type=F32) * scale
        weights = jnp.exp(scores - jnp.max(scores, axis=-1, keepdims=True))
        probs = weights * (1.0 / jnp.sum(weights, axis=-1, keepdims=True))
        probs_low = probs.astype(BF16)
        new_out = both(jnp.dot(probs_low, values, preferred_element_type=F32))
        grad_probs = lax.dot_general(grad, values, NT, preferred_element_type=F32)
        inner = jnp.sum(probs * grad_probs, axis=-1, keepdims=True)
        grad_scores = (probs * (grad_probs - inner) * scale).astype(BF16)
        new_grad = both(jnp.dot(grad_scores, keys, preferred_element_type=F32))
        for n in range(2):
            probs_kept[2 * b + n] = probs_low[:, n * NBLEN : (n + 1) * NBLEN]
            scores_kept[2 * b + n] = grad_scores[:, n * NBLEN : (n + 1) * NBLEN]
        here = pl.ds(pl.multiple_of(b * BLOCK, BLOCK), BLOCK)
        out[here, :] = jnp.where(is_last, new_out, last_out).astype(BF16)
        query_grads[here, :] = jnp.where(is_last, new_grad, last_grad).astype(BF16)
        return new_out, new_grad

    zeros = jnp.zeros((BLOCK, PAIR), F32)
    lax.fori_loop(0, blocks, step, (zeros, zeros), unroll=2)


def slot_pass(order, fresh, last, wide_q, wide_g, probs_kept, scores_kept, running, sums, slot_grads):
    sums[...] = jnp.zeros_like(sums)

    def step(u, carry):
        use = order[u]
        block = lax.div(use, 2)
        starts = fresh[u] == 1
        for part, (kept, wide) in enumerate(((scores_kept, wide_q), (probs_kept, wide_g))):
            new = lax.dot_general(kept[use], wide[block], TN, preferred_element_type=F32)
            new = jnp.where(starts, 0.0, sums[part]) + new
            sums[part] = new
            running[u, part] = new.astype(BF16)
        return carry

    def pick(s, carry):
        slot_grads[s] = running[last[s]]
        return carry

    lax.fori_loop(0, order.shape[0], step, 0, unroll=2)
    lax.fori_loop(0, slot_grads.shape[0], pick, 0)


def everything_kernel(
    enc_count, seq_count, chunks,
    entries, slots, order, fresh, last, queries, grads, pool, context, grad_queries, returned,
    *scratch,
):
    take = iter(scratch)
    per_chunk = [[next(take) for _ in range(8)] for _ in range(chunks)]
    wide_q, wide_g, probs_kept, scores_kept, running, sums = [next(take) for _ in range(6)]
    pool_sems, send_sems, recv_sems = [next(take) for _ in range(3)]

    enc_here, seq_here = lax.axis_index("enc"), lax.axis_index("seq")
    rows = queries.shape[0]
    width = pool.shape[-1]
    mine = pl.ds(pl.multiple_of(seq_here * rows, rows), rows)

    def peer_of(here, k, count):
        return lax.rem(here + k, count)

    loads = []
    for c in range(chunks):
        own = per_chunk[c][0]
        loads.append(pltpu.make_async_copy(pool.at[:, :, :, pl.ds(c * PAIR, PAIR)], own, pool_sems.at[c]))
        loads[-1].start()

    barrier = pltpu.get_barrier_semaphore()

    def greet_enc(k, carry):
        pl.semaphore_signal(
            barrier, inc=1, device_id={"enc": peer_of(enc_here, k, enc_count)}, device_id_type=MESH
        )
        return carry

    def greet_seq(k, carry):
        pl.semaphore_signal(
            barrier, inc=1, device_id={"seq": peer_of(seq_here, k, seq_count)}, device_id_type=MESH
        )
        return carry

    lax.fori_loop(1, enc_count, greet_enc, 0)
    lax.fori_loop(1, seq_count, greet_seq, 0)

    def pick(c):
        loads[c].wait()
        own, outgoing = per_chunk[c][0], per_chunk[c][1]

        def body(e, carry):
            outgoing[e] = own[entries[e]]
            return carry

        lax.fori_loop(0, enc_count, body, 0)

    def exchange(group, axis, here, count, source_of, target_of):
        def body(k, carry):
            peer = peer_of(here, k, count)
            pltpu.make_async_remote_copy(
                src_ref=source_of(peer),
                dst_ref=target_of(here),
                send_sem=send_sems.at[group],
                recv_sem=recv_sems.at[group],
                device_id={axis: peer},
                device_id_type=MESH,
            ).start()
            return carry

        lax.fori_loop(1, count, body, 0)
        pltpu.make_async_copy(source_of(here), target_of(here), recv_sems.at[group]).start()

    def cut(c, p):
        return pl.ds(pl.multiple_of(p * width + c * PAIR, PAIR), PAIR)

    def token_rows(p):
        return pl.ds(pl.multiple_of(p * rows, rows), rows)

    def fetch(c):
        own, outgoing, arrived = per_chunk[c][:3]
        exchange(6 * c, "enc", enc_here, enc_count, lambda p: outgoing.at[p], lambda p: arrived.at[p])

    def to_heads(c):
        head_queries, head_grads = per_chunk[c][3:5]
        for n, (source, target) in enumerate(((queries, head_queries), (grads, head_grads))):
            exchange(
                6 * c + 1 + n, "seq", seq_here, seq_count,
                lambda p, source=source: source.at[:, cut(c, p)],
                lambda p, target=target: target.at[token_rows(p), :],
            )

    def to_tokens(c):
        out, query_grads = per_chunk[c][5:7]
        for n, (source, target) in enumerate(((out, context), (query_grads, grad_queries))):
            exchange(
                6 * c + 3 + n, "seq", seq_here, seq_count,
                lambda p, source=source: source.at[token_rows(p), :],
                lambda p, target=target: target.at[:, cut(c, p)],
            )

    def give_back(c):
        slot_grads = per_chunk[c][7]
        exchange(
            6 * c + 5, "enc", enc_here, enc_count,
            lambda p: slot_grads.at[p], lambda p: returned.at[c, p],
        )

    def whole(ref, sem):
        pltpu.make_async_copy(ref, ref, sem).wait()

    def sent(group, ref, count):
        part = ref.at[pl.ds(0, ref.shape[0] // count * (count - 1))]
        whole(part, send_sems.at[group])

    def arrive(group, ref):
        whole(ref, recv_sems.at[group])

    def compute(c):
        _, _, arrived, head_queries, head_grads, out, query_grads, slot_grads = per_chunk[c]
        arrive(6 * c, arrived)
        arrive(6 * c + 1, head_queries)
        arrive(6 * c + 2, head_grads)
        block_pass(
            slots, head_queries, head_grads, arrived, out, query_grads,
            wide_q, wide_g, probs_kept, scores_kept,
        )
        to_tokens(c)
        slot_pass(
            order, fresh, last, wide_q, wide_g, probs_kept, scores_kept, running, sums, slot_grads
        )

    pick(0)
    pl.semaphore_wait(barrier, enc_count + seq_count - 2)
    fetch(0)
    to_heads(0)
    for c in range(1, chunks):
        pick(c)
    for c in range(chunks):
        sent(6 * c, per_chunk[c][1], enc_count)
        if c + 1 < chunks:
            fetch(c + 1)
            to_heads(c + 1)
        if c > 0:
            give_back(c - 1)
        compute(c)
    give_back(chunks - 1)

    for c in range(chunks):
        _, _, arrived, head_queries, head_grads, out, query_grads, slot_grads = per_chunk[c]
        sent(6 * c + 1, head_queries, seq_count)
        sent(6 * c + 2, head_grads, seq_count)
        sent(6 * c + 3, out, seq_count)
        sent(6 * c + 4, query_grads, seq_count)
        sent(6 * c + 5, slot_grads, enc_count)
        arrive(6 * c + 3, out)
        arrive(6 * c + 4, query_grads)
        arrive(6 * c + 5, slot_grads)


def everything(enc_count, seq_count, entries, slots, order, fresh, last, queries, grads, pool):
    rows = queries.shape[0]
    held, _, _, width = pool.shape
    chunks = width // PAIR
    length = rows * seq_count
    blocks = length // BLOCK
    tokens = jax.ShapeDtypeStruct(queries.shape, queries.dtype)

    def entry_buffer(count):
        return pltpu.VMEM((count, 2, NBLEN, PAIR), BF16)

    heads = pltpu.VMEM((length, PAIR), BF16)
    chunk_shapes = [
        entry_buffer(held), entry_buffer(enc_count), entry_buffer(enc_count),
        heads, heads, heads, heads, entry_buffer(enc_count),
    ]
    return pl.pallas_call(
        functools.partial(everything_kernel, enc_count, seq_count, chunks),
        out_shape=(
            tokens,
            tokens,
            jax.ShapeDtypeStruct((chunks, enc_count, 2, NBLEN, PAIR), pool.dtype),
        ),
        in_specs=[SCALAR] * 5 + [ANY] * 3,
        out_specs=(ANY, ANY, ANY),
        scratch_shapes=chunk_shapes * chunks
        + [
            pltpu.VMEM((blocks, 2 * BLOCK, PAIR), BF16),
            pltpu.VMEM((blocks, 2 * BLOCK, PAIR), BF16),
            pltpu.VMEM((2 * blocks, 2 * BLOCK, NBLEN), BF16),
            pltpu.VMEM((2 * blocks, 2 * BLOCK, NBLEN), BF16),
            pltpu.VMEM((2 * blocks, 2, NBLEN, PAIR), BF16),
            pltpu.VMEM((2, NBLEN, PAIR), F32),
            pltpu.SemaphoreType.DMA((chunks,)),
            pltpu.SemaphoreType.DMA((6 * chunks,)),
            pltpu.SemaphoreType.DMA((6 * chunks,)),
        ],
        compiler_params=pltpu.CompilerParams(
            collective_id=0, has_side_effects=True, vmem_limit_bytes=56 * MIB
        ),
    )(entries, slots, order, fresh, last, queries, grads, pool)


def owner_kernel(entries, returned, context, grad_queries, pool_grads, context_out, grad_out, total, sems):
    moves = [
        pltpu.make_async_copy(context, context_out, sems.at[0]),
        pltpu.make_async_copy(grad_queries, grad_out, sems.at[1]),
    ]
    step_here = pl.program_id(0) * pl.num_programs(1) + pl.program_id(1)

    @pl.when(step_here == 0)
    def _():
        for move in moves:
            move.start()

    total[...] = jnp.zeros_like(total)

    def step(e, carry):
        total[entries[e]] += returned[e].astype(F32)
        return carry

    lax.fori_loop(0, returned.shape[0], step, 0)
    pool_grads[...] = total[...].astype(pool_grads.dtype)

    @pl.when(step_here == pl.num_programs(0) * pl.num_programs(1) - 1)
    def _():
        for move in moves:
            move.wait()


def owner_sum(entries, returned, context, grad_queries, pool_shape):
    cuts = 2
    chunks, count, two, length, width = returned.shape
    part = length // cuts
    tokens = jax.ShapeDtypeStruct(context.shape, context.dtype)
    return pl.pallas_call(
        owner_kernel,
        out_shape=(jax.ShapeDtypeStruct(pool_shape, returned.dtype), tokens, tokens),
        grid=(chunks, cuts),
        in_specs=[
            SCALAR,
            pl.BlockSpec((None, count, two, part, width), lambda c, i: (c, 0, 0, i, 0)),
            ANY,
            ANY,
        ],
        out_specs=(pl.BlockSpec((pool_shape[0], two, part, width), lambda c, i: (0, 0, i, c)), ANY, ANY),
        scratch_shapes=[
            pltpu.VMEM((pool_shape[0], two, part, width), F32),
            pltpu.SemaphoreType.DMA((2,)),
        ],
        compiler_params=pltpu.CompilerParams(vmem_limit_bytes=58 * MIB),
    )(entries, returned, context, grad_queries)


def local(enc_count, seq_count, queries, kv_pool, send_lists, block_slots, grad_context):
    entries = send_lists.reshape(-1)
    slots = block_slots.reshape(-1)
    order, fresh, last = sort_uses(slots, enc_count)
    context, grad_queries, returned = everything(
        enc_count, seq_count, entries, slots, order, fresh, last, queries[0], grad_context[0], kv_pool
    )
    pool_grads, context, grad_queries = owner_sum(
        entries, returned, context, grad_queries, kv_pool.shape
    )
    return context[None], grad_queries[None], pool_grads


def solution(mesh):
    in_specs = (
        P("enc", "seq", None),
        P("enc", None, None, "seq"),
        P("enc", None, None),
        P("enc", None, None),
        P("enc", "seq", None),
    )
    out_specs = (P("enc", "seq", None), P("enc", "seq", None), P("enc", None, None, "seq"))
    body = functools.partial(local, mesh.shape["enc"], mesh.shape["seq"])
    return jax.shard_map(body, mesh=mesh, in_specs=in_specs, out_specs=out_specs, check_vma=False)
```

time: 264 us -> 330 us (1.25)
  Pallas kernels: 255 us -> 328 us
  local copies, waits for them, and re-layouts: 8.23 us -> 1.38 us
    pallas_call x1, Pallas kernels: 4.43 us -> 130 us  [owner_sum(): pl.pallas_call(owner_kernel, out_shape=(jax.ShapeDtypeStruct(pool_shape,...]
    pallas_call x3 -> x2, Pallas kernels: 251 us -> 198 us  [the longest x1 195 us: everything(): pl.pallas_call(functools.partial(everything_kernel, enc_count, seq_count,...]
    unnamed x13 -> x1, local copies, waits for them, and re-layouts: 8.13 us -> 0.76 us
where the time goes in v2:
time: 330 us
  Pallas kernels  328 us (99%)
    pallas_call x1, Pallas kernels, everything(): pl.pallas_call(functools.partial(everything_kernel, enc_count, seq_count,...  195 us
    pallas_call x1, Pallas kernels, owner_sum(): pl.pallas_call(owner_kernel, out_shape=(jax.ShapeDtypeStruct(pool_shape,...  130 us

profile of v2, /device:TPU:1, one launch (start us, length us, event | category | flops | bytes accessed | tf_op | source)
XLA Modules:
  0.0 329.9 jit_solution(3837773068975579738)
XLA Ops:
  0.6 0.8 copy.9
  1.4 0.6 reshape.13.slots
  2.0 2.7 shard_map.76
  4.7 195.0 %shard_map.77 = (bf16[128,8192]{1,0:T(8,128)(2,1)}, bf16[128,8192]{1,0:T(8,128)(2,1)}, bf16[2,16,2,128,256]{4,3,2,1,0:T(8,128)(2,1)}) custom-call(s32[16]{0:T(128)} %bitcast.7, s32[64]{0:T(128)} %reshape.13.slots, s32[64]{0:T(128)} %get-tuple-element.12.order, s32[64]{0:T(128)} %get-tuple-element.13.fresh, s32[16]{0:T(128)} %get-tuple-element.14.last, ...), custom_call_target="tpu_custom_call" | custom-call | tf_op jit(solution)/shard_map/pallas_call | solution.py:309
  199.7 130.2 %shard_map.78 = (bf16[8,2,128,512]{3,2,1,0:T(8,128)(2,1)}, bf16[128,8192]{1,0:T(8,128)(2,1)}, bf16[128,8192]{1,0:T(8,128)(2,1)}) custom-call(s32[16]{0:T(128)} %bitcast.8, bf16[2,16,2,128,256]{4,3,2,1,0:T(8,128)(2,1)} %get-tuple-element.15.returned, bf16[128,8192]{1,0:T(8,128)(2,1)} %get-tuple-element.16.context, ...), custom_call_target="tpu_custom_call" | custom-call | tf_op jit(solution)/shard_map/pallas_call | solution.py:368

commit v3 on v2

--- a/solution.py
+++ b/solution.py
@@ -21,50 +21,36 @@
 BF16 = jnp.bfloat16
 
 
-def sort_kernel(slots, order, fresh, last, count):
-    uses, entries = slots.shape[0], last.shape[0]
-
-    def clear(s, carry):
-        count[s] = 0
-        return carry
-
-    def tally(u, carry):
-        count[slots[u]] += 1
-        fresh[u] = 0
-        return carry
-
-    def starts(s, begin):
-        size = count[s]
-        count[s] = begin
-        last[s] = begin + size - 1
-        fresh[begin] = 1
-        return begin + size
-
-    def place(u, carry):
-        slot = slots[u]
-        order[count[slot]] = u
-        count[slot] += 1
-        return carry
-
-    lax.fori_loop(0, entries, clear, 0)
-    lax.fori_loop(0, uses, tally, 0)
-    lax.fori_loop(0, entries, starts, 0)
-    lax.fori_loop(0, uses, place, 0)
-
-
-def sort_uses(slots, entries):
-    uses = slots.shape[0]
-    return pl.pallas_call(
-        sort_kernel,
-        out_shape=(
-            jax.ShapeDtypeStruct((uses,), jnp.int32),
-            jax.ShapeDtypeStruct((uses,), jnp.int32),
-            jax.ShapeDtypeStruct((entries,), jnp.int32),
-        ),
-        in_specs=[SCALAR],
-        out_specs=(SCALAR,) * 3,
-        scratch_shapes=[pltpu.SMEM((entries,), jnp.int32)],
-    )(slots)
+def sort_uses(slots, rank_ref, ranks, sem):
+    neighbours, blocks = slots.shape
+    uses = neighbours * blocks
+    lane = lax.broadcasted_iota(jnp.int32, (uses, 128), 1)
+    row = lax.broadcasted_iota(jnp.int32, (uses, 128), 0)
+    along_lanes = jnp.full((uses, 128), uses * 128, jnp.int32)
+    along_rows = jnp.zeros((uses, 128), jnp.int32)
+    slot_rows = jnp.zeros((uses, 128), jnp.int32)
+    for n in range(neighbours):
+
+        def put(b, carry, n=n):
+            along_lanes, along_rows, slot_rows = carry
+            use = n * blocks + b
+            key = slots[n, b] * uses + use
+            along_lanes = jnp.where(lane == use, key, along_lanes)
+            along_rows = jnp.where(row == use, key, along_rows)
+            slot_rows = jnp.where(row == use, slots[n, b], slot_rows)
+            return along_lanes, along_rows, slot_rows
+
+        along_lanes, along_rows, slot_rows = lax.fori_loop(
+            0, blocks, put, (along_lanes, along_rows, slot_rows)
+        )
+    rank = jnp.sum((along_lanes < along_rows).astype(jnp.int32), axis=1, keepdims=True)
+    order = jnp.sum(jnp.where(rank == lane, row, 0), axis=0, keepdims=True)
+    ends = jnp.sum((slot_rows <= lane).astype(jnp.int32), axis=0, keepdims=True) - 1
+    rank_ref[0:1, :] = order
+    rank_ref[1:2, :] = ends
+    copy = pltpu.make_async_copy(rank_ref, ranks, sem)
+    copy.start()
+    copy.wait()
 
 
 def block_pass(slots, queries, grads, received, out, query_grads, wide_q, wide_g, probs_kept, scores_kept):
@@ -87,7 +73,7 @@
 
     def step(b, carry):
         last_out, last_grad = carry
-        first, second = slots[2 * b], slots[2 * b + 1]
+        first, second = slots[0, b], slots[1, b]
         query, grad = moved(queries, b), moved(grads, b)
         wide_q[b] = query
         wide_g[b] = grad
@@ -103,8 +89,8 @@
         grad_scores = (probs * (grad_probs - inner) * scale).astype(BF16)
         new_grad = both(jnp.dot(grad_scores, keys, preferred_element_type=F32))
         for n in range(2):
-            probs_kept[2 * b + n] = probs_low[:, n * NBLEN : (n + 1) * NBLEN]
-            scores_kept[2 * b + n] = grad_scores[:, n * NBLEN : (n + 1) * NBLEN]
+            probs_kept[n * blocks + b] = probs_low[:, n * NBLEN : (n + 1) * NBLEN]
+            scores_kept[n * blocks + b] = grad_scores[:, n * NBLEN : (n + 1) * NBLEN]
         here = pl.ds(pl.multiple_of(b * BLOCK, BLOCK), BLOCK)
         out[here, :] = jnp.where(is_last, new_out, last_out).astype(BF16)
         query_grads[here, :] = jnp.where(is_last, new_grad, last_grad).astype(BF16)
@@ -114,37 +100,39 @@
     lax.fori_loop(0, blocks, step, (zeros, zeros), unroll=2)
 
 
-def slot_pass(order, fresh, last, wide_q, wide_g, probs_kept, scores_kept, running, sums, slot_grads):
+def slot_pass(slots, ranks, wide_q, wide_g, probs_kept, scores_kept, running, sums, slot_grads):
+    neighbours, blocks = slots.shape
     sums[...] = jnp.zeros_like(sums)
 
-    def step(u, carry):
-        use = order[u]
-        block = lax.div(use, 2)
-        starts = fresh[u] == 1
+    def step(u, before):
+        use = ranks[0, u]
+        neighbour = lax.div(use, blocks)
+        block = use - neighbour * blocks
+        slot = slots[neighbour, block]
         for part, (kept, wide) in enumerate(((scores_kept, wide_q), (probs_kept, wide_g))):
             new = lax.dot_general(kept[use], wide[block], TN, preferred_element_type=F32)
-            new = jnp.where(starts, 0.0, sums[part]) + new
+            new = jnp.where(slot != before, 0.0, sums[part]) + new
             sums[part] = new
             running[u, part] = new.astype(BF16)
+        return slot
+
+    def pick(s, carry):
+        slot_grads[s] = running[ranks[1, s]]
         return carry
 
-    def pick(s, carry):
-        slot_grads[s] = running[last[s]]
-        return carry
-
-    lax.fori_loop(0, order.shape[0], step, 0, unroll=2)
+    lax.fori_loop(0, neighbours * blocks, step, -1, unroll=2)
     lax.fori_loop(0, slot_grads.shape[0], pick, 0)
 
 
 def everything_kernel(
     enc_count, seq_count, chunks,
-    entries, slots, order, fresh, last, queries, grads, pool, context, grad_queries, returned,
+    entries, slots, queries, grads, pool, context, grad_queries, returned,
     *scratch,
 ):
     take = iter(scratch)
     per_chunk = [[next(take) for _ in range(8)] for _ in range(chunks)]
     wide_q, wide_g, probs_kept, scores_kept, running, sums = [next(take) for _ in range(6)]
-    pool_sems, send_sems, recv_sems = [next(take) for _ in range(3)]
+    rank_ref, ranks, pool_sems, send_sems, recv_sems, rank_sem = [next(take) for _ in range(6)]
 
     enc_here, seq_here = lax.axis_index("enc"), lax.axis_index("seq")
     rows = queries.shape[0]
@@ -259,7 +247,7 @@
         )
         to_tokens(c)
         slot_pass(
-            order, fresh, last, wide_q, wide_g, probs_kept, scores_kept, running, sums, slot_grads
+            slots, ranks, wide_q, wide_g, probs_kept, scores_kept, running, sums, slot_grads
         )
 
     pick(0)
@@ -268,6 +256,7 @@
     to_heads(0)
     for c in range(1, chunks):
         pick(c)
+    sort_uses(slots, rank_ref, ranks, rank_sem.at[0])
     for c in range(chunks):
         sent(6 * c, per_chunk[c][1], enc_count)
         if c + 1 < chunks:
@@ -290,7 +279,7 @@
         arrive(6 * c + 5, slot_grads)
 
 
-def everything(enc_count, seq_count, entries, slots, order, fresh, last, queries, grads, pool):
+def everything(enc_count, seq_count, entries, slots, queries, grads, pool):
     rows = queries.shape[0]
     held, _, _, width = pool.shape
     chunks = width // PAIR
@@ -313,7 +302,7 @@
             tokens,
             jax.ShapeDtypeStruct((chunks, enc_count, 2, NBLEN, PAIR), pool.dtype),
         ),
-        in_specs=[SCALAR] * 5 + [ANY] * 3,
+        in_specs=[SCALAR] * 2 + [ANY] * 3,
         out_specs=(ANY, ANY, ANY),
         scratch_shapes=chunk_shapes * chunks
         + [
@@ -323,28 +312,22 @@
             pltpu.VMEM((2 * blocks, 2 * BLOCK, NBLEN), BF16),
             pltpu.VMEM((2 * blocks, 2, NBLEN, PAIR), BF16),
             pltpu.VMEM((2, NBLEN, PAIR), F32),
+            pltpu.VMEM((8, 128), jnp.int32),
+            pltpu.SMEM((8, 128), jnp.int32),
             pltpu.SemaphoreType.DMA((chunks,)),
             pltpu.SemaphoreType.DMA((6 * chunks,)),
             pltpu.SemaphoreType.DMA((6 * chunks,)),
+            pltpu.SemaphoreType.DMA((1,)),
         ],
         compiler_params=pltpu.CompilerParams(
             collective_id=0, has_side_effects=True, vmem_limit_bytes=56 * MIB
         ),
-    )(entries, slots, order, fresh, last, queries, grads, pool)
-
-
-def owner_kernel(entries, returned, context, grad_queries, pool_grads, context_out, grad_out, total, sems):
-    moves = [
-        pltpu.make_async_copy(context, context_out, sems.at[0]),
-        pltpu.make_async_copy(grad_queries, grad_out, sems.at[1]),
-    ]
-    step_here = pl.program_id(0) * pl.num_programs(1) + pl.program_id(1)
-
-    @pl.when(step_here == 0)
-    def _():
-        for move in moves:
-            move.start()
-
+    )(entries, slots, queries, grads, pool)
+
+
+def owner_kernel(entries, returned, context, grad_queries, pool_grads, context_out, grad_out, total):
+    context_out[...] = context[...]
+    grad_out[...] = grad_queries[...]
     total[...] = jnp.zeros_like(total)
 
     def step(e, carry):
@@ -353,18 +336,15 @@
 
     lax.fori_loop(0, returned.shape[0], step, 0)
     pool_grads[...] = total[...].astype(pool_grads.dtype)
-
-    @pl.when(step_here == pl.num_programs(0) * pl.num_programs(1) - 1)
-    def _():
-        for move in moves:
-            move.wait()
 
 
 def owner_sum(entries, returned, context, grad_queries, pool_shape):
     cuts = 2
     chunks, count, two, length, width = returned.shape
     part = length // cuts
+    rows, columns = context.shape
     tokens = jax.ShapeDtypeStruct(context.shape, context.dtype)
+    token_block = pl.BlockSpec((rows, columns // (chunks * cuts)), lambda c, i: (0, c * cuts + i))
     return pl.pallas_call(
         owner_kernel,
         out_shape=(jax.ShapeDtypeStruct(pool_shape, returned.dtype), tokens, tokens),
@@ -372,24 +352,24 @@
         in_specs=[
             SCALAR,
             pl.BlockSpec((None, count, two, part, width), lambda c, i: (c, 0, 0, i, 0)),
-            ANY,
-            ANY,
+            token_block,
+            token_block,
         ],
-        out_specs=(pl.BlockSpec((pool_shape[0], two, part, width), lambda c, i: (0, 0, i, c)), ANY, ANY),
-        scratch_shapes=[
-            pltpu.VMEM((pool_shape[0], two, part, width), F32),
-            pltpu.SemaphoreType.DMA((2,)),
-        ],
+        out_specs=(
+            pl.BlockSpec((pool_shape[0], two, part, width), lambda c, i: (0, 0, i, c)),
+            token_block,
+            token_block,
+        ),
+        scratch_shapes=[pltpu.VMEM((pool_shape[0], two, part, width), F32)],
         compiler_params=pltpu.CompilerParams(vmem_limit_bytes=58 * MIB),
     )(entries, returned, context, grad_queries)
 
 
 def local(enc_count, seq_count, queries, kv_pool, send_lists, block_slots, grad_context):
     entries = send_lists.reshape(-1)
-    slots = block_slots.reshape(-1)
-    order, fresh, last = sort_uses(slots, enc_count)
+    slots = block_slots[0].T
     context, grad_queries, returned = everything(
-        enc_count, seq_count, entries, slots, order, fresh, last, queries[0], grad_context[0], kv_pool
+        enc_count, seq_count, entries, slots, queries[0], grad_context[0], kv_pool
     )
     pool_grads, context, grad_queries = owner_sum(
         entries, returned, context, grad_queries, kv_pool.shape

time: 330 us -> 203 us (0.62)
  Pallas kernels: 328 us -> 202 us
    pallas_call x1, Pallas kernels: 130 us -> 6.93 us  [owner_sum(): pl.pallas_call(owner_kernel, out_shape=(jax.ShapeDtypeStruct(pool_shape,...]
where the time goes in v3:
time: 203 us
  Pallas kernels  202 us (100%)
    pallas_call x1, Pallas kernels, everything(): pl.pallas_call(functools.partial(everything_kernel, enc_count, seq_count,...  195 us
    pallas_call x1, Pallas kernels, owner_sum(): pl.pallas_call(owner_kernel, out_shape=(jax.ShapeDtypeStruct(pool_shape,...  6.93 us

profile of v3, /device:TPU:1, one launch (start us, length us, event | category | flops | bytes accessed | tf_op | source)
XLA Modules:
  0.0 202.5 jit_solution(4098161167556303720)
XLA Ops:
  0.6 195.0 %shard_map.76 = (bf16[128,8192]{1,0:T(8,128)(2,1)}, bf16[128,8192]{1,0:T(8,128)(2,1)}, bf16[2,16,2,128,256]{4,3,2,1,0:T(8,128)(2,1)}) custom-call(s32[16]{0:T(128)} %bitcast.10, s32[2,32]{1,0:T(2,128)} %bitcast.12, bf16[128,8192]{1,0:T(8,128)(2,1)} %bitcast.8, bf16[128,8192]{1,0:T(8,128)(2,1)} %bitcast.9, bf16[8,2,128,512]{3,2,1,0:T(8,128)(2,1)} %pool.1), custom_call_target="tpu_custom_call" | custom-call | tf_op jit(solution)/shard_map/pallas_call | solution.py:298
  195.6 6.9 %shard_map.77 = (bf16[8,2,128,512]{3,2,1,0:T(8,128)(2,1)}, bf16[128,8192]{1,0:T(8,128)(2,1)}, bf16[128,8192]{1,0:T(8,128)(2,1)}) custom-call(s32[16]{0:T(128)} %bitcast.11, bf16[2,16,2,128,256]{4,3,2,1,0:T(8,128)(2,1)} %get-tuple-element.9.returned, bf16[128,8192]{1,0:T(8,128)(2,1)} %get-tuple-element.10.context, ...), custom_call_target="tpu_custom_call" | custom-call | tf_op jit(solution)/shard_map/pallas_call | solution.py:348

commit v4 on v3

--- a/solution.py
+++ b/solution.py
@@ -13,6 +13,7 @@
 PAIR = 2 * DH
 MESH = pl.DeviceIdType.MESH
 ANY = pl.BlockSpec(memory_space=pl.ANY)
+IN_VMEM = pl.BlockSpec(memory_space=pltpu.VMEM)
 SCALAR = pl.BlockSpec(memory_space=pltpu.SMEM)
 MIB = 1 << 20
 NT = (((1,), (1,)), ((), ()))
@@ -21,7 +22,7 @@
 BF16 = jnp.bfloat16
 
 
-def sort_uses(slots, rank_ref, ranks, sem):
+def sort_uses(slots, rank_ref, first_row):
     neighbours, blocks = slots.shape
     uses = neighbours * blocks
     lane = lax.broadcasted_iota(jnp.int32, (uses, 128), 1)
@@ -46,11 +47,8 @@
     rank = jnp.sum((along_lanes < along_rows).astype(jnp.int32), axis=1, keepdims=True)
     order = jnp.sum(jnp.where(rank == lane, row, 0), axis=0, keepdims=True)
     ends = jnp.sum((slot_rows <= lane).astype(jnp.int32), axis=0, keepdims=True) - 1
-    rank_ref[0:1, :] = order
-    rank_ref[1:2, :] = ends
-    copy = pltpu.make_async_copy(rank_ref, ranks, sem)
-    copy.start()
-    copy.wait()
+    rank_ref[first_row : first_row + 1, :] = order
+    rank_ref[first_row + 1 : first_row + 2, :] = ends
 
 
 def block_pass(slots, queries, grads, received, out, query_grads, wide_q, wide_g, probs_kept, scores_kept):
@@ -124,13 +122,29 @@
     lax.fori_loop(0, slot_grads.shape[0], pick, 0)
 
 
+def owner_pass(entries, ranks, returned, running, sums, store):
+    def step(place, before):
+        sender = ranks[2, place]
+        entry = entries[0, sender]
+        for part in range(2):
+            new = returned[sender, part].astype(F32)
+            new = jnp.where(entry != before, 0.0, sums[part]) + new
+            sums[part] = new
+            running[place, part] = new.astype(BF16)
+        return entry
+
+    sums[...] = jnp.zeros_like(sums)
+    lax.fori_loop(0, entries.shape[1], step, -1)
+    store(lambda entry: running[ranks[3, entry]])
+
+
 def everything_kernel(
     enc_count, seq_count, chunks,
-    entries, slots, queries, grads, pool, context, grad_queries, returned,
+    entries, slots, queries, grads, pool, context, grad_queries, pool_grads,
     *scratch,
 ):
     take = iter(scratch)
-    per_chunk = [[next(take) for _ in range(8)] for _ in range(chunks)]
+    per_chunk = [[next(take) for _ in range(9)] for _ in range(chunks)]
     wide_q, wide_g, probs_kept, scores_kept, running, sums = [next(take) for _ in range(6)]
     rank_ref, ranks, pool_sems, send_sems, recv_sems, rank_sem = [next(take) for _ in range(6)]
 
@@ -170,13 +184,14 @@
         own, outgoing = per_chunk[c][0], per_chunk[c][1]
 
         def body(e, carry):
-            outgoing[e] = own[entries[e]]
+            outgoing[e] = own[entries[0, e]]
             return carry
 
         lax.fori_loop(0, enc_count, body, 0)
 
     def exchange(group, axis, here, count, source_of, target_of):
-        def body(k, carry):
+        def body(i, carry):
+            k = count // 2 + (1 - 2 * lax.rem(i, 2)) * lax.div(i + 1, 2)
             peer = peer_of(here, k, count)
             pltpu.make_async_remote_copy(
                 src_ref=source_of(peer),
@@ -188,7 +203,7 @@
             ).start()
             return carry
 
-        lax.fori_loop(1, count, body, 0)
+        lax.fori_loop(0, count - 1, body, 0)
         pltpu.make_async_copy(source_of(here), target_of(here), recv_sems.at[group]).start()
 
     def cut(c, p):
@@ -220,10 +235,10 @@
             )
 
     def give_back(c):
-        slot_grads = per_chunk[c][7]
+        slot_grads, returned = per_chunk[c][7:9]
         exchange(
             6 * c + 5, "enc", enc_here, enc_count,
-            lambda p: slot_grads.at[p], lambda p: returned.at[c, p],
+            lambda p: slot_grads.at[p], lambda p: returned.at[p],
         )
 
     def whole(ref, sem):
@@ -237,7 +252,7 @@
         whole(ref, recv_sems.at[group])
 
     def compute(c):
-        _, _, arrived, head_queries, head_grads, out, query_grads, slot_grads = per_chunk[c]
+        _, _, arrived, head_queries, head_grads, out, query_grads, slot_grads, returned = per_chunk[c]
         arrive(6 * c, arrived)
         arrive(6 * c + 1, head_queries)
         arrive(6 * c + 2, head_grads)
@@ -256,7 +271,11 @@
     to_heads(0)
     for c in range(1, chunks):
         pick(c)
-    sort_uses(slots, rank_ref, ranks, rank_sem.at[0])
+    sort_uses(slots, rank_ref, 0)
+    sort_uses(entries, rank_ref, 2)
+    copy = pltpu.make_async_copy(rank_ref, ranks, rank_sem.at[0])
+    copy.start()
+    copy.wait()
     for c in range(chunks):
         sent(6 * c, per_chunk[c][1], enc_count)
         if c + 1 < chunks:
@@ -268,7 +287,7 @@
     give_back(chunks - 1)
 
     for c in range(chunks):
-        _, _, arrived, head_queries, head_grads, out, query_grads, slot_grads = per_chunk[c]
+        _, _, arrived, head_queries, head_grads, out, query_grads, slot_grads, returned = per_chunk[c]
         sent(6 * c + 1, head_queries, seq_count)
         sent(6 * c + 2, head_grads, seq_count)
         sent(6 * c + 3, out, seq_count)
@@ -276,7 +295,16 @@
         sent(6 * c + 5, slot_grads, enc_count)
         arrive(6 * c + 3, out)
         arrive(6 * c + 4, query_grads)
-        arrive(6 * c + 5, slot_grads)
+        arrive(6 * c + 5, returned)
+
+        def store(value, c=c):
+            def body(entry, carry):
+                pool_grads[entry, :, :, c * PAIR : (c + 1) * PAIR] = value(entry)
+                return carry
+
+            lax.fori_loop(0, pool_grads.shape[0], body, 0)
+
+        owner_pass(entries, ranks, returned, running, sums, store)
 
 
 def everything(enc_count, seq_count, entries, slots, queries, grads, pool):
@@ -285,7 +313,7 @@
     chunks = width // PAIR
     length = rows * seq_count
     blocks = length // BLOCK
-    tokens = jax.ShapeDtypeStruct(queries.shape, queries.dtype)
+    tokens = pltpu.VMEM(queries.shape, queries.dtype)
 
     def entry_buffer(count):
         return pltpu.VMEM((count, 2, NBLEN, PAIR), BF16)
@@ -293,17 +321,17 @@
     heads = pltpu.VMEM((length, PAIR), BF16)
     chunk_shapes = [
         entry_buffer(held), entry_buffer(enc_count), entry_buffer(enc_count),
-        heads, heads, heads, heads, entry_buffer(enc_count),
+        heads, heads, heads, heads, entry_buffer(enc_count), entry_buffer(enc_count),
     ]
     return pl.pallas_call(
         functools.partial(everything_kernel, enc_count, seq_count, chunks),
         out_shape=(
             tokens,
             tokens,
-            jax.ShapeDtypeStruct((chunks, enc_count, 2, NBLEN, PAIR), pool.dtype),
+            pltpu.VMEM(pool.shape, pool.dtype),
         ),
         in_specs=[SCALAR] * 2 + [ANY] * 3,
-        out_specs=(ANY, ANY, ANY),
+        out_specs=(ANY, ANY, IN_VMEM),
         scratch_shapes=chunk_shapes * chunks
         + [
             pltpu.VMEM((blocks, 2 * BLOCK, PAIR), BF16),
@@ -320,59 +348,16 @@
             pltpu.SemaphoreType.DMA((1,)),
         ],
         compiler_params=pltpu.CompilerParams(
-            collective_id=0, has_side_effects=True, vmem_limit_bytes=56 * MIB
+            collective_id=0, has_side_effects=True, vmem_limit_bytes=54 * MIB
         ),
     )(entries, slots, queries, grads, pool)
 
 
-def owner_kernel(entries, returned, context, grad_queries, pool_grads, context_out, grad_out, total):
-    context_out[...] = context[...]
-    grad_out[...] = grad_queries[...]
-    total[...] = jnp.zeros_like(total)
-
-    def step(e, carry):
-        total[entries[e]] += returned[e].astype(F32)
-        return carry
-
-    lax.fori_loop(0, returned.shape[0], step, 0)
-    pool_grads[...] = total[...].astype(pool_grads.dtype)
-
-
-def owner_sum(entries, returned, context, grad_queries, pool_shape):
-    cuts = 2
-    chunks, count, two, length, width = returned.shape
-    part = length // cuts
-    rows, columns = context.shape
-    tokens = jax.ShapeDtypeStruct(context.shape, context.dtype)
-    token_block = pl.BlockSpec((rows, columns // (chunks * cuts)), lambda c, i: (0, c * cuts + i))
-    return pl.pallas_call(
-        owner_kernel,
-        out_shape=(jax.ShapeDtypeStruct(pool_shape, returned.dtype), tokens, tokens),
-        grid=(chunks, cuts),
-        in_specs=[
-            SCALAR,
-            pl.BlockSpec((None, count, two, part, width), lambda c, i: (c, 0, 0, i, 0)),
-            token_block,
-            token_block,
-        ],
-        out_specs=(
-            pl.BlockSpec((pool_shape[0], two, part, width), lambda c, i: (0, 0, i, c)),
-            token_block,
-            token_block,
-        ),
-        scratch_shapes=[pltpu.VMEM((pool_shape[0], two, part, width), F32)],
-        compiler_params=pltpu.CompilerParams(vmem_limit_bytes=58 * MIB),
-    )(entries, returned, context, grad_queries)
-
-
 def local(enc_count, seq_count, queries, kv_pool, send_lists, block_slots, grad_context):
-    entries = send_lists.reshape(-1)
+    entries = send_lists.reshape(1, -1)
     slots = block_slots[0].T
-    context, grad_queries, returned = everything(
+    context, grad_queries, pool_grads = everything(
         enc_count, seq_count, entries, slots, queries[0], grad_context[0], kv_pool
-    )
-    pool_grads, context, grad_queries = owner_sum(
-        entries, returned, context, grad_queries, kv_pool.shape
     )
     return context[None], grad_queries[None], pool_grads
 

time: 203 us -> 198 us (0.975)
  Pallas kernels: 202 us -> 193 us
  local copies, waits for them, and re-layouts: 0 us -> 3.96 us
    pallas_call x1 -> x0, Pallas kernels: 6.93 us -> none  [owner_sum(): pl.pallas_call(owner_kernel, out_shape=(jax.ShapeDtypeStruct(pool_shape,...]
    unnamed x0 -> x3, local copies, waits for them, and re-layouts: none -> 3.96 us
    pallas_call x1, Pallas kernels: 195 us -> 193 us  [everything(): pl.pallas_call(functools.partial(everything_kernel, enc_count, seq_count,...]
where the time goes in v4:
time: 198 us; the launch traced here: 197 us
  Pallas kernels  193 us (97%)
  local copies, waits for them, and re-layouts  3.96 us (2%)
    pallas_call x1, Pallas kernels, everything(): pl.pallas_call(functools.partial(everything_kernel, enc_count, seq_count,...  193 us

profile of v4, /device:TPU:1, one launch (start us, length us, event | category | flops | bytes accessed | tf_op | source)
XLA Modules:
  0.0 197.4 jit_solution(15061953431795646844)
XLA Ops:
  0.6 192.8 %shard_map.76 = (bf16[128,8192]{1,0:T(8,128)(2,1)S(1)}, bf16[128,8192]{1,0:T(8,128)(2,1)S(1)}, bf16[8,2,128,512]{3,2,1,0:T(8,128)(2,1)S(1)}) custom-call(s32[1,16]{1,0:T(1,128)} %bitcast.13, s32[2,32]{1,0:T(2,128)} %bitcast.12, bf16[128,8192]{1,0:T(8,128)(2,1)} %bitcast.10, bf16[128,8192]{1,0:T(8,128)(2,1)} %bitcast.11, bf16[8,2,128,512]{3,2,1,0:T(8,128)(2,1)} %pool.1), custom_call_target="tpu_custom_call" | custom-call | tf_op jit(solution)/shard_map/pallas_call | solution.py:326
  193.4 1.3 copy.11
  194.8 1.3 copy.12
  196.1 1.3 copy.13

commit v5 on v4

--- a/solution.py
+++ b/solution.py
@@ -140,11 +140,12 @@
 
 def everything_kernel(
     enc_count, seq_count, chunks,
-    entries, slots, queries, grads, pool, context, grad_queries, pool_grads,
+    entries, slots, queries, grads, pool, context, grad_queries, early_sums, last_returned,
     *scratch,
 ):
     take = iter(scratch)
-    per_chunk = [[next(take) for _ in range(9)] for _ in range(chunks)]
+    per_chunk = [[next(take) for _ in range(9)] for _ in range(chunks - 1)]
+    per_chunk.append([next(take) for _ in range(8)] + [last_returned])
     wide_q, wide_g, probs_kept, scores_kept, running, sums = [next(take) for _ in range(6)]
     rank_ref, ranks, pool_sems, send_sems, recv_sems, rank_sem = [next(take) for _ in range(6)]
 
@@ -297,14 +298,16 @@
         arrive(6 * c + 4, query_grads)
         arrive(6 * c + 5, returned)
 
-        def store(value, c=c):
-            def body(entry, carry):
-                pool_grads[entry, :, :, c * PAIR : (c + 1) * PAIR] = value(entry)
-                return carry
-
-            lax.fori_loop(0, pool_grads.shape[0], body, 0)
-
-        owner_pass(entries, ranks, returned, running, sums, store)
+        if c + 1 < chunks:
+
+            def store(value, c=c):
+                def body(entry, carry):
+                    early_sums[c, entry] = value(entry)
+                    return carry
+
+                lax.fori_loop(0, pool.shape[0], body, 0)
+
+            owner_pass(entries, ranks, returned, running, sums, store)
 
 
 def everything(enc_count, seq_count, entries, slots, queries, grads, pool):
@@ -328,11 +331,13 @@
         out_shape=(
             tokens,
             tokens,
-            pltpu.VMEM(pool.shape, pool.dtype),
+            pltpu.VMEM((chunks - 1, held, 2, NBLEN, PAIR), pool.dtype),
+            pltpu.VMEM((enc_count, 2, NBLEN, PAIR), pool.dtype),
         ),
         in_specs=[SCALAR] * 2 + [ANY] * 3,
-        out_specs=(ANY, ANY, IN_VMEM),
-        scratch_shapes=chunk_shapes * chunks
+        out_specs=(ANY, ANY, IN_VMEM, IN_VMEM),
+        scratch_shapes=chunk_shapes * (chunks - 1)
+        + chunk_shapes[:8]
         + [
             pltpu.VMEM((blocks, 2 * BLOCK, PAIR), BF16),
             pltpu.VMEM((blocks, 2 * BLOCK, PAIR), BF16),
@@ -353,11 +358,62 @@
     )(entries, slots, queries, grads, pool)
 
 
+def finish_kernel(
+    entries, context, grad_queries, early_sums, returned, context_out, grad_out, pool_grads, total, low, sems
+):
+    early = early_sums.shape[0]
+    last = pl.ds(early * PAIR, PAIR)
+    moves = [
+        pltpu.make_async_copy(context, context_out, sems.at[0]),
+        pltpu.make_async_copy(grad_queries, grad_out, sems.at[1]),
+    ]
+    for c in range(early):
+        moves.append(
+            pltpu.make_async_copy(
+                early_sums.at[c], pool_grads.at[:, :, :, pl.ds(c * PAIR, PAIR)], sems.at[3 + c]
+            )
+        )
+    for move in moves:
+        move.start()
+    total[...] = jnp.zeros_like(total)
+
+    def step(e, carry):
+        total[entries[0, e]] += returned[e].astype(F32)
+        return carry
+
+    lax.fori_loop(0, returned.shape[0], step, 0)
+    low[...] = total[...].astype(BF16)
+    moves.append(pltpu.make_async_copy(low, pool_grads.at[:, :, :, last], sems.at[2]))
+    moves[-1].start()
+    for move in moves:
+        move.wait()
+
+
+def finish(entries, context, grad_queries, early_sums, returned, pool_shape):
+    tokens = jax.ShapeDtypeStruct(context.shape, context.dtype)
+    part = pool_shape[:-1] + (PAIR,)
+    return pl.pallas_call(
+        finish_kernel,
+        out_shape=(tokens, tokens, jax.ShapeDtypeStruct(pool_shape, BF16)),
+        in_specs=[SCALAR] + [IN_VMEM] * 4,
+        out_specs=(ANY, ANY, ANY),
+        scratch_shapes=[
+            pltpu.VMEM(part, F32),
+            pltpu.VMEM(part, BF16),
+            pltpu.SemaphoreType.DMA((3 + early_sums.shape[0],)),
+        ],
+        compiler_params=pltpu.CompilerParams(vmem_limit_bytes=16 * MIB),
+    )(entries, context, grad_queries, early_sums, returned)
+
+
 def local(enc_count, seq_count, queries, kv_pool, send_lists, block_slots, grad_context):
     entries = send_lists.reshape(1, -1)
     slots = block_slots[0].T
-    context, grad_queries, pool_grads = everything(
+    context, grad_queries, early_sums, returned = everything(
         enc_count, seq_count, entries, slots, queries[0], grad_context[0], kv_pool
+    )
+    context, grad_queries, pool_grads = finish(
+        entries, context, grad_queries, early_sums, returned, kv_pool.shape
     )
     return context[None], grad_queries[None], pool_grads
 

time: 198 us -> 196 us (0.990)
  local copies, waits for them, and re-layouts: 3.96 us -> 0.01 us
  Pallas kernels: 193 us -> 195 us
    unnamed x3 -> x2, local copies, waits for them, and re-layouts: 3.96 us -> 0.01 us
    pallas_call x0 -> x1, Pallas kernels: none -> 3.24 us  [finish(): pl.pallas_call(finish_kernel, out_shape=(tokens, tokens, jax.ShapeDtypeSt...]
where the time goes in v5:
time: 196 us
  Pallas kernels  195 us (99%)
    pallas_call x1, Pallas kernels, everything(): pl.pallas_call(functools.partial(everything_kernel, enc_count, seq_count,...  192 us

profile of v5, /device:TPU:1, one launch (start us, length us, event | category | flops | bytes accessed | tf_op | source)
XLA Modules:
  0.0 196.0 jit_solution(15063301482962845082)
XLA Ops:
  0.6 0.0 copy-start
  0.6 192.1 %shard_map.76 = (bf16[128,8192]{1,0:T(8,128)(2,1)S(1)}, bf16[128,8192]{1,0:T(8,128)(2,1)S(1)}, bf16[1,8,2,128,256]{4,3,2,1,0:T(8,128)(2,1)S(1)}, bf16[16,2,128,256]{3,2,1,0:T(8,128)(2,1)S(1)}) custom-call(s32[1,16]{1,0:T(1,128)} %bitcast.8, s32[2,32]{1,0:T(2,128)} %bitcast.12, bf16[128,8192]{1,0:T(8,128)(2,1)} %bitcast.10, bf16[128,8192]{1,0:T(8,128)(2,1)} %bitcast.11, ...), custom_call_target="tpu_custom_call" | custom-call | tf_op jit(solution)/shard_map/pallas_call | solution.py:329
  192.7 0.0 copy-done
  192.7 3.2 %shard_map.77 = (bf16[128,8192]{1,0:T(8,128)(2,1)}, bf16[128,8192]{1,0:T(8,128)(2,1)}, bf16[8,2,128,512]{3,2,1,0:T(8,128)(2,1)}) custom-call(s32[1,16]{1,0:T(1,128)S(1)} %bitcast.9, bf16[128,8192]{1,0:T(8,128)(2,1)S(1)} %get-tuple-element.10.context, bf16[128,8192]{1,0:T(8,128)(2,1)S(1)} %get-tuple-element.11.grad_queries, ...), custom_call_target="tpu_custom_call" | custom-call | tf_op jit(solution)/shard_map/pallas_call | solution.py:395
Async XLA Ops:
  0.6 192.1 %copy-start = (s32[1,16,1]{1,2,0:T(1,128)S(1)}, s32[1,16,1]{1,2,0:T(1,128)}, u32[]{:S(2)}) copy-start(s32[1,16,1]{1,2,0:T(1,128)} %param.7) | copy-start | bytes 196

commit v6 on v5

--- a/solution.py
+++ b/solution.py
@@ -16,6 +16,7 @@
 IN_VMEM = pl.BlockSpec(memory_space=pltpu.VMEM)
 SCALAR = pl.BlockSpec(memory_space=pltpu.SMEM)
 MIB = 1 << 20
+SPLIT = 1
 NT = (((1,), (1,)), ((), ()))
 TN = (((0,), (0,)), ((), ()))
 F32 = jnp.float32
@@ -79,7 +80,7 @@
         values = jnp.concatenate([received[first, 1], received[second, 1]], axis=0)
         scores = lax.dot_general(query, keys, NT, preferred_element_type=F32) * scale
         weights = jnp.exp(scores - jnp.max(scores, axis=-1, keepdims=True))
-        probs = weights * (1.0 / jnp.sum(weights, axis=-1, keepdims=True))
+        probs = weights / jnp.sum(weights, axis=-1, keepdims=True)
         probs_low = probs.astype(BF16)
         new_out = both(jnp.dot(probs_low, values, preferred_element_type=F32))
         grad_probs = lax.dot_general(grad, values, NT, preferred_element_type=F32)
@@ -109,6 +110,7 @@
         slot = slots[neighbour, block]
         for part, (kept, wide) in enumerate(((scores_kept, wide_q), (probs_kept, wide_g))):
             new = lax.dot_general(kept[use], wide[block], TN, preferred_element_type=F32)
+            new = new.astype(BF16).astype(F32)
             new = jnp.where(slot != before, 0.0, sums[part]) + new
             sums[part] = new
             running[u, part] = new.astype(BF16)
@@ -353,54 +355,59 @@
             pltpu.SemaphoreType.DMA((1,)),
         ],
         compiler_params=pltpu.CompilerParams(
-            collective_id=0, has_side_effects=True, vmem_limit_bytes=54 * MIB
+            collective_id=0, has_side_effects=True, vmem_limit_bytes=48 * MIB
         ),
     )(entries, slots, queries, grads, pool)
 
 
 def finish_kernel(
-    entries, context, grad_queries, early_sums, returned, context_out, grad_out, pool_grads, total, low, sems
+    entries_far, context, grad_queries, early_sums, returned, context_out, grad_out, pool_grads,
+    entries, total, low, sems,
 ):
     early = early_sums.shape[0]
-    last = pl.ds(early * PAIR, PAIR)
-    moves = [
-        pltpu.make_async_copy(context, context_out, sems.at[0]),
-        pltpu.make_async_copy(grad_queries, grad_out, sems.at[1]),
-    ]
+    moves = []
+
+    def move(source, target):
+        moves.append(pltpu.make_async_copy(source, target, sems.at[len(moves)]))
+        moves[-1].start()
+
+    move(entries_far, entries)
+    half = context.shape[0] // SPLIT
+    for source, target in ((context, context_out), (grad_queries, grad_out)):
+        for n in range(SPLIT):
+            rows = pl.ds(n * half, half)
+            move(source.at[rows, :], target.at[rows, :])
     for c in range(early):
-        moves.append(
-            pltpu.make_async_copy(
-                early_sums.at[c], pool_grads.at[:, :, :, pl.ds(c * PAIR, PAIR)], sems.at[3 + c]
-            )
-        )
-    for move in moves:
-        move.start()
+        move(early_sums.at[c], pool_grads.at[:, :, :, pl.ds(c * PAIR, PAIR)])
     total[...] = jnp.zeros_like(total)
-
-    def step(e, carry):
-        total[entries[0, e]] += returned[e].astype(F32)
-        return carry
-
-    lax.fori_loop(0, returned.shape[0], step, 0)
-    low[...] = total[...].astype(BF16)
-    moves.append(pltpu.make_async_copy(low, pool_grads.at[:, :, :, last], sems.at[2]))
-    moves[-1].start()
-    for move in moves:
-        move.wait()
+    moves.pop(0).wait()
+    moves.insert(0, None)
+    for part in range(2):
+
+        def step(e, carry, part=part):
+            total[part, entries[0, e]] += returned[e, part].astype(F32)
+            return carry
+
+        lax.fori_loop(0, returned.shape[0], step, 0)
+        low[part] = total[part].astype(BF16)
+        move(low.at[part], pool_grads.at[:, part, :, pl.ds(early * PAIR, PAIR)])
+    for one in moves[1:]:
+        one.wait()
 
 
 def finish(entries, context, grad_queries, early_sums, returned, pool_shape):
     tokens = jax.ShapeDtypeStruct(context.shape, context.dtype)
-    part = pool_shape[:-1] + (PAIR,)
+    part = (pool_shape[1], pool_shape[0], pool_shape[2], PAIR)
     return pl.pallas_call(
         finish_kernel,
         out_shape=(tokens, tokens, jax.ShapeDtypeStruct(pool_shape, BF16)),
-        in_specs=[SCALAR] + [IN_VMEM] * 4,
+        in_specs=[ANY] + [IN_VMEM] * 4,
         out_specs=(ANY, ANY, ANY),
         scratch_shapes=[
+            pltpu.SMEM(entries.shape, entries.dtype),
             pltpu.VMEM(part, F32),
             pltpu.VMEM(part, BF16),
-            pltpu.SemaphoreType.DMA((3 + early_sums.shape[0],)),
+            pltpu.SemaphoreType.DMA((3 + 2 * SPLIT + early_sums.shape[0],)),
         ],
         compiler_params=pltpu.CompilerParams(vmem_limit_bytes=16 * MIB),
     )(entries, context, grad_queries, early_sums, returned)

time: 196 us -> 196 us (level)
  no operation moved by 1% of the time
where the time goes in v6:
time: 196 us; the launch traced here: 195 us
  Pallas kernels  195 us (99%)
    pallas_call x1, Pallas kernels, everything(): pl.pallas_call(functools.partial(everything_kernel, enc_count, seq_count,...  192 us

profile of v6, /device:TPU:1, one launch (start us, length us, event | category | flops | bytes accessed | tf_op | source)
XLA Modules:
  0.0 195.4 jit_solution(16424567970589032369)
XLA Ops:
  0.6 0.0 copy-start
  0.6 192.1 %shard_map.76 = (bf16[128,8192]{1,0:T(8,128)(2,1)S(1)}, bf16[128,8192]{1,0:T(8,128)(2,1)S(1)}, bf16[1,8,2,128,256]{4,3,2,1,0:T(8,128)(2,1)S(1)}, bf16[16,2,128,256]{3,2,1,0:T(8,128)(2,1)S(1)}) custom-call(s32[1,16]{1,0:T(1,128)} %bitcast.8, s32[2,32]{1,0:T(2,128)} %bitcast.12, bf16[128,8192]{1,0:T(8,128)(2,1)} %bitcast.10, bf16[128,8192]{1,0:T(8,128)(2,1)} %bitcast.11, ...), custom_call_target="tpu_custom_call" | custom-call | tf_op jit(solution)/shard_map/pallas_call | solution.py:331
  192.7 0.0 copy-done
  192.7 2.7 %shard_map.77 = (bf16[128,8192]{1,0:T(8,128)(2,1)}, bf16[128,8192]{1,0:T(8,128)(2,1)}, bf16[8,2,128,512]{3,2,1,0:T(8,128)(2,1)}) custom-call(s32[1,16]{1,0:T(1,128)S(1)} %bitcast.9, bf16[128,8192]{1,0:T(8,128)(2,1)S(1)} %get-tuple-element.10.context, bf16[128,8192]{1,0:T(8,128)(2,1)S(1)} %get-tuple-element.11.grad_queries, ...), custom_call_target="tpu_custom_call" | custom-call | tf_op jit(solution)/shard_map/pallas_call | solution.py:401
Async XLA Ops:
  0.6 192.1 %copy-start = (s32[1,16,1]{1,2,0:T(1,128)S(1)}, s32[1,16,1]{1,2,0:T(1,128)}, u32[]{:S(2)}) copy-start(s32[1,16,1]{1,2,0:T(1,128)} %param.7) | copy-start | bytes 196

commit v7 on v6

--- a/solution.py
+++ b/solution.py
@@ -142,7 +142,7 @@
 
 def everything_kernel(
     enc_count, seq_count, chunks,
-    entries, slots, queries, grads, pool, context, grad_queries, early_sums, last_returned,
+    entries_far, slots_far, queries, grads, pool, context, grad_queries, early_sums, last_returned,
     *scratch,
 ):
     take = iter(scratch)
@@ -150,6 +150,7 @@
     per_chunk.append([next(take) for _ in range(8)] + [last_returned])
     wide_q, wide_g, probs_kept, scores_kept, running, sums = [next(take) for _ in range(6)]
     rank_ref, ranks, pool_sems, send_sems, recv_sems, rank_sem = [next(take) for _ in range(6)]
+    entries, slots, list_sems = [next(take) for _ in range(3)]
 
     enc_here, seq_here = lax.axis_index("enc"), lax.axis_index("seq")
     rows = queries.shape[0]
@@ -165,6 +166,12 @@
         loads.append(pltpu.make_async_copy(pool.at[:, :, :, pl.ds(c * PAIR, PAIR)], own, pool_sems.at[c]))
         loads[-1].start()
 
+    lists = [
+        pltpu.make_async_copy(entries_far, entries, list_sems.at[0]),
+        pltpu.make_async_copy(slots_far, slots, list_sems.at[1]),
+    ]
+    for one in lists:
+        one.start()
     barrier = pltpu.get_barrier_semaphore()
 
     def greet_enc(k, carry):
@@ -268,6 +275,8 @@
             slots, ranks, wide_q, wide_g, probs_kept, scores_kept, running, sums, slot_grads
         )
 
+    for one in lists:
+        one.wait()
     pick(0)
     pl.semaphore_wait(barrier, enc_count + seq_count - 2)
     fetch(0)
@@ -336,7 +345,7 @@
             pltpu.VMEM((chunks - 1, held, 2, NBLEN, PAIR), pool.dtype),
             pltpu.VMEM((enc_count, 2, NBLEN, PAIR), pool.dtype),
         ),
-        in_specs=[SCALAR] * 2 + [ANY] * 3,
+        in_specs=[ANY] * 5,
         out_specs=(ANY, ANY, IN_VMEM, IN_VMEM),
         scratch_shapes=chunk_shapes * (chunks - 1)
         + chunk_shapes[:8]
@@ -353,6 +362,9 @@
             pltpu.SemaphoreType.DMA((6 * chunks,)),
             pltpu.SemaphoreType.DMA((6 * chunks,)),
             pltpu.SemaphoreType.DMA((1,)),
+            pltpu.SMEM(entries.shape, entries.dtype),
+            pltpu.SMEM(slots.shape, slots.dtype),
+            pltpu.SemaphoreType.DMA((2,)),
         ],
         compiler_params=pltpu.CompilerParams(
             collective_id=0, has_side_effects=True, vmem_limit_bytes=48 * MIB

time: 196 us -> 195 us (level)
  no operation moved by 1% of the time
where the time goes in v7:
time: 195 us
  Pallas kernels  194 us (99%)
    pallas_call x1, Pallas kernels, everything(): pl.pallas_call(functools.partial(everything_kernel, enc_count, seq_count,...  191 us

profile of v7, /device:TPU:1, one launch (start us, length us, event | category | flops | bytes accessed | tf_op | source)
XLA Modules:
  0.0 194.8 jit_solution(11664566586116150648)
XLA Ops:
  0.6 0.0 copy-start
  0.6 191.4 %shard_map.76 = (bf16[128,8192]{1,0:T(8,128)(2,1)S(1)}, bf16[128,8192]{1,0:T(8,128)(2,1)S(1)}, bf16[1,8,2,128,256]{4,3,2,1,0:T(8,128)(2,1)S(1)}, bf16[16,2,128,256]{3,2,1,0:T(8,128)(2,1)S(1)}) custom-call(s32[1,16]{1,0:T(1,128)} %bitcast.8, s32[2,32]{1,0:T(2,128)} %bitcast.12, bf16[128,8192]{1,0:T(8,128)(2,1)} %bitcast.10, bf16[128,8192]{1,0:T(8,128)(2,1)} %bitcast.11, ...), custom_call_target="tpu_custom_call" | custom-call | tf_op jit(solution)/shard_map/pallas_call | solution.py:340
  192.0 0.0 copy-done
  192.1 2.7 %shard_map.77 = (bf16[128,8192]{1,0:T(8,128)(2,1)}, bf16[128,8192]{1,0:T(8,128)(2,1)}, bf16[8,2,128,512]{3,2,1,0:T(8,128)(2,1)}) custom-call(s32[1,16]{1,0:T(1,128)S(1)} %bitcast.9, bf16[128,8192]{1,0:T(8,128)(2,1)S(1)} %get-tuple-element.10.context, bf16[128,8192]{1,0:T(8,128)(2,1)S(1)} %get-tuple-element.11.grad_queries, ...), custom_call_target="tpu_custom_call" | custom-call | tf_op jit(solution)/shard_map/pallas_call | solution.py:413
Async XLA Ops:
  0.6 191.4 %copy-start = (s32[1,16,1]{1,2,0:T(1,128)S(1)}, s32[1,16,1]{1,2,0:T(1,128)}, u32[]{:S(2)}) copy-start(s32[1,16,1]{1,2,0:T(1,128)} %param.7) | copy-start | bytes 196

commit v8 on v7

--- a/solution.py
+++ b/solution.py
@@ -160,34 +160,38 @@
     def peer_of(here, k, count):
         return lax.rem(here + k, count)
 
-    loads = []
-    for c in range(chunks):
-        own = per_chunk[c][0]
-        loads.append(pltpu.make_async_copy(pool.at[:, :, :, pl.ds(c * PAIR, PAIR)], own, pool_sems.at[c]))
-        loads[-1].start()
-
+    def far_first(i, count):
+        return count // 2 + (1 - 2 * lax.rem(i, 2)) * lax.div(i + 1, 2)
+
+    barrier = pltpu.get_barrier_semaphore()
+
+    def greet_enc(i, carry):
+        k = far_first(i, enc_count)
+        pl.semaphore_signal(
+            barrier, inc=1, device_id={"enc": peer_of(enc_here, k, enc_count)}, device_id_type=MESH
+        )
+        return carry
+
+    def greet_seq(i, carry):
+        k = far_first(i, seq_count)
+        pl.semaphore_signal(
+            barrier, inc=1, device_id={"seq": peer_of(seq_here, k, seq_count)}, device_id_type=MESH
+        )
+        return carry
+
+    lax.fori_loop(0, enc_count - 1, greet_enc, 0)
     lists = [
         pltpu.make_async_copy(entries_far, entries, list_sems.at[0]),
         pltpu.make_async_copy(slots_far, slots, list_sems.at[1]),
     ]
     for one in lists:
         one.start()
-    barrier = pltpu.get_barrier_semaphore()
-
-    def greet_enc(k, carry):
-        pl.semaphore_signal(
-            barrier, inc=1, device_id={"enc": peer_of(enc_here, k, enc_count)}, device_id_type=MESH
-        )
-        return carry
-
-    def greet_seq(k, carry):
-        pl.semaphore_signal(
-            barrier, inc=1, device_id={"seq": peer_of(seq_here, k, seq_count)}, device_id_type=MESH
-        )
-        return carry
-
-    lax.fori_loop(1, enc_count, greet_enc, 0)
-    lax.fori_loop(1, seq_count, greet_seq, 0)
+    loads = []
+    for c in range(chunks):
+        own = per_chunk[c][0]
+        loads.append(pltpu.make_async_copy(pool.at[:, :, :, pl.ds(c * PAIR, PAIR)], own, pool_sems.at[c]))
+        loads[-1].start()
+    lax.fori_loop(0, seq_count - 1, greet_seq, 0)
 
     def pick(c):
         loads[c].wait()
@@ -201,7 +205,7 @@
 
     def exchange(group, axis, here, count, source_of, target_of):
         def body(i, carry):
-            k = count // 2 + (1 - 2 * lax.rem(i, 2)) * lax.div(i + 1, 2)
+            k = far_first(i, count)
             peer = peer_of(here, k, count)
             pltpu.make_async_remote_copy(
                 src_ref=source_of(peer),

time: 195 us -> 195 us (level)
  no operation moved by 1% of the time
where the time goes in v8:
time: 195 us
  Pallas kernels  194 us (99%)
    pallas_call x1, Pallas kernels, everything(): pl.pallas_call(functools.partial(everything_kernel, enc_count, seq_count,...  191 us

profile of v8, /device:TPU:1, one launch (start us, length us, event | category | flops | bytes accessed | tf_op | source)
XLA Modules:
  0.0 194.8 jit_solution(12533258507732556202)
XLA Ops:
  0.6 0.0 copy-start
  0.6 191.5 %shard_map.76 = (bf16[128,8192]{1,0:T(8,128)(2,1)S(1)}, bf16[128,8192]{1,0:T(8,128)(2,1)S(1)}, bf16[1,8,2,128,256]{4,3,2,1,0:T(8,128)(2,1)S(1)}, bf16[16,2,128,256]{3,2,1,0:T(8,128)(2,1)S(1)}) custom-call(s32[1,16]{1,0:T(1,128)} %bitcast.8, s32[2,32]{1,0:T(2,128)} %bitcast.12, bf16[128,8192]{1,0:T(8,128)(2,1)} %bitcast.10, bf16[128,8192]{1,0:T(8,128)(2,1)} %bitcast.11, ...), custom_call_target="tpu_custom_call" | custom-call | tf_op jit(solution)/shard_map/pallas_call | solution.py:344
  192.1 0.0 copy-done
  192.1 2.7 %shard_map.77 = (bf16[128,8192]{1,0:T(8,128)(2,1)}, bf16[128,8192]{1,0:T(8,128)(2,1)}, bf16[8,2,128,512]{3,2,1,0:T(8,128)(2,1)}) custom-call(s32[1,16]{1,0:T(1,128)S(1)} %bitcast.9, bf16[128,8192]{1,0:T(8,128)(2,1)S(1)} %get-tuple-element.10.context, bf16[128,8192]{1,0:T(8,128)(2,1)S(1)} %get-tuple-element.11.grad_queries, ...), custom_call_target="tpu_custom_call" | custom-call | tf_op jit(solution)/shard_map/pallas_call | solution.py:417
Async XLA Ops:
  0.6 191.5 %copy-start = (s32[1,16,1]{1,2,0:T(1,128)S(1)}, s32[1,16,1]{1,2,0:T(1,128)}, u32[]{:S(2)}) copy-start(s32[1,16,1]{1,2,0:T(1,128)} %param.7) | copy-start | bytes 196
